TPU v7x, 32 devices: a whole 2x2x4 slice. The times are simulated.
32 devices in a mesh: slab: 8 (over y, x, core), grp: 4 (over z).
Axes of the slice: x: 2, y: 2, z: 4, core: 2. Of those that a mesh axis runs over, the one named last changes fastest.
Arguments:
- volume: float32 [64, 32, 16, 128], P(None, 'slab', 'grp'), may hold values from -6 to 6
- conv_fine: float32 [3, 3, 3, 64, 64], replicated, may hold values from -0.15625 to 0.15625
- down_first: float32 [2, 2, 2, 64, 128], replicated, may hold values from -0.25 to 0.25
- conv_middle: float32 [3, 3, 3, 128, 128], replicated, may hold values from -0.109375 to 0.109375
- down_second: float32 [2, 2, 2, 128, 256], P(None, None, None, None, 'grp'), may hold values from -0.1875 to 0.1875
- conv_coarse: float32 [3, 3, 3, 256, 512], P(None, None, None, None, 'grp'), may hold values from -0.078125 to 0.078125
Outputs:
- features: float32 [512, 8, 128], P('grp', 'slab')
All inputs are finite; a program needn't handle non-finite values.
Results may differ from a plain program's by a relative error of at most 0.000082.
Values sent between devices are 32-bit elements; how exact they have to be, the bound alone decides.
A program may use at most 64 MiB of HBM per device.

v0:
```python
import jax
import jax.numpy as jnp
from jax import lax
from jax.sharding import PartitionSpec as P


def padded_2(cells, sides, width):
    for axis, dim in sides:
        count = lax.axis_size(axis)
        ends = count - 1
        head = lax.slice_in_dim(cells, 0, width, axis=dim)
        tail = lax.slice_in_dim(cells, cells.shape[dim] - width, cells.shape[dim], axis=dim)
        cells = jnp.concatenate(
            [
                lax.ppermute(tail, axis, [(i, (i + 1) % count) for i in range(ends)]),
                cells,
                lax.ppermute(head, axis, [((i + 1) % count, i) for i in range(ends)]),
            ],
            axis=dim,
        )
    return cells


def from_behind(shard, axis, by):
    peers = lax.axis_size(axis)
    pairs = [(i, i + by) for i in range(peers) if 0 <= i + by < peers]
    return lax.ppermute(shard, axis, pairs)


def convolve(field, kernel, stride, padding):
    return lax.conv_general_dilated(
        field[None],
        kernel,
        (stride, stride, stride),
        padding,
        dimension_numbers=("NCDHW", "DHWIO", "NCDHW"),
        precision=lax.Precision.HIGHEST,
    )[0]


def per_device(volume, conv_fine, down_first, conv_middle, down_second, conv_coarse):
    valid = ((0, 0), (0, 0), (0, 0))
    sideways = ((0, 0), (0, 0), (1, 1))
    padded = padded_2(volume, (("slab", 1), ("grp", 2)), 1)
    level_one = jax.nn.gelu(convolve(padded, conv_fine, 1, sideways), approximate=False)
    level_two = convolve(level_one, down_first, 2, valid)
    padded_two = padded_2(level_two, (("slab", 1), ("grp", 2)), 1)
    level_two = jax.nn.gelu(convolve(padded_two, conv_middle, 1, sideways), approximate=False)
    gathered = lax.all_gather(level_two, "grp", axis=2, tiled=True)
    shares = convolve(gathered, down_second, 2, valid)
    coarse = lax.all_gather(shares, "grp", axis=0, tiled=True)
    planar = ((0, 0), (1, 1), (1, 1))
    summed = convolve(coarse, conv_coarse, 1, ((1, 1), (1, 1), (1, 1)))
    upward = convolve(coarse[:, -1:], conv_coarse[0:1], 1, planar)
    downward = convolve(coarse[:, :1], conv_coarse[2:3], 1, planar)
    from_lower = from_behind(upward, "slab", 1)
    from_upper = from_behind(downward, "slab", -1)
    summed = summed.at[:, :1].add(from_lower)
    summed = summed.at[:, -1:].add(from_upper)
    result = jax.nn.gelu(summed, approximate=False)
    return result.reshape(result.shape[0], result.shape[1], result.shape[2] * result.shape[3])


def solution(mesh):
    placed = (
        P(None, "slab", "grp", None),
        P(),
        P(),
        P(),
        P(None, None, None, None, "grp"),
        P(None, None, None, None, "grp"),
    )
    return jax.shard_map(
        per_device, mesh=mesh, in_specs=placed, out_specs=P("grp", "slab", None), check_vma=False
    )
```

profile of v0, /device:TPU:1, one launch (start us, length us, event | category | flops | bytes accessed | tf_op | source)
XLA Modules:
  0.0 121.6 jit_solution(17833059538798822995)
XLA Ops:
  0.0 0.0 copy-start
  0.0 1.1 fusion.97
  1.2 4.5 %collective-permute-start = (f32[64,1,4,128]{3,0,2,1:T(8,128)S(1)}, f32[64,1,4,128]{3,0,2,1:T(8,128)S(1)}, u32[]{:S(2)}, u32[]{:S(2)}) collective-permute-start(f32[64,1,4,128]{3,0,2,1:T(8,128)S(1)} %copy.117), channel_id=1, source_target_pairs={{0,4},{4,8},{8,12},{12,16},{16,20},{20,24},{24,28},{1,5},{5,9},{9,... | collective-permute-start | bytes 393224 | tf_op jit(solution)/shard_map/ppermute | solution.py:15
  5.7 1.9 %collective-permute-start.1 = (f32[64,1,4,128]{3,0,2,1:T(8,128)S(1)}, f32[64,1,4,128]{3,0,2,1:T(8,128)S(1)}, u32[]{:S(2)}, u32[]{:S(2)}) collective-permute-start(f32[64,1,4,128]{3,0,2,1:T(8,128)S(1)} %copy.118), channel_id=1, source_target_pairs={{4,0},{8,4},{12,8},{16,12},{20,16},{24,20},{28,24},{5,1},{9,5},{13... | collective-permute-start | bytes 393224 | tf_op jit(solution)/shard_map/ppermute | solution.py:17
  7.6 0.0 collective-permute-done
  7.6 0.0 copy-done.2
  7.7 0.2 constant_dynamic-update-slice_fusion.1
  7.8 4.2 %collective-permute-done.1 = f32[64,1,4,128]{3,0,2,1:T(8,128)S(1)} collective-permute-done((f32[64,1,4,128]{3,0,2,1:T(8,128)S(1)}, f32[64,1,4,128]{3,0,2,1:T(8,128)S(1)}, u32[]{:S(2)}, u32[]{:S(2)}) %collective-permute-start.1) | collective-permute-done | bytes 131104 | tf_op jit(solution)/shard_map/ppermute | solution.py:17
  12.0 3.2 %collective-permute-start.2 = (f32[64,6,1,128]{3,0,2,1:T(8,128)S(1)}, f32[64,6,1,128]{3,0,2,1:T(8,128)S(1)}, u32[]{:S(2)}, u32[]{:S(2)}) collective-permute-start(f32[64,6,1,128]{3,0,2,1:T(8,128)S(1)} %get-tuple-element.45), channel_id=1, source_target_pairs={{0,1},{1,2},{2,3},{4,5},{5,6},{6,7},{8,9},{9,10},{10,11},{12,13},{... | collective-permute-start | bytes 589832 | tf_op jit(solution)/shard_map/ppermute | solution.py:15
  15.2 1.3 %collective-permute-start.3 = (f32[64,6,1,128]{3,0,2,1:T(8,128)S(1)}, f32[64,6,1,128]{3,0,2,1:T(8,128)S(1)}, u32[]{:S(2)}, u32[]{:S(2)}) collective-permute-start(f32[64,6,1,128]{3,0,2,1:T(8,128)S(1)} %get-tuple-element.46), channel_id=1, source_target_pairs={{1,0},{2,1},{3,2},{5,4},{6,5},{7,6},{9,8},{10,9},{11,10},{13,12},{... | collective-permute-start | bytes 589832 | tf_op jit(solution)/shard_map/ppermute | solution.py:17
  16.5 1.3 %collective-permute-done.2 = f32[64,6,1,128]{3,0,2,1:T(8,128)S(1)} collective-permute-done((f32[64,6,1,128]{3,0,2,1:T(8,128)S(1)}, f32[64,6,1,128]{3,0,2,1:T(8,128)S(1)}, u32[]{:S(2)}, u32[]{:S(2)}) %collective-permute-start.2) | collective-permute-done | bytes 196640 | tf_op jit(solution)/shard_map/ppermute | solution.py:15
  17.8 3.8 %collective-permute-done.3 = f32[64,6,1,128]{3,0,2,1:T(8,128)S(1)} collective-permute-done((f32[64,6,1,128]{3,0,2,1:T(8,128)S(1)}, f32[64,6,1,128]{3,0,2,1:T(8,128)S(1)}, u32[]{:S(2)}, u32[]{:S(2)}) %collective-permute-start.3) | collective-permute-done | bytes 196640 | tf_op jit(solution)/shard_map/ppermute | solution.py:17
  21.7 0.1 maximum_bitcast_fusion
  21.8 4.2 %copy.106 = f32[64,6,6,1,128]{0,3,4,2,1:T(1,128)} copy(f32[64,6,6,1,128]{4,0,2,1,3:T(8,128)S(1)} %maximum_bitcast_fusion) | data formatting | bytes 2359296
  26.0 3.4 %pad.6.clone = f32[64,6,6,1,136]{0,3,4,2,1:T(1,128)S(1)} pad(f32[64,6,6,1,128]{0,3,4,2,1:T(1,128)} %copy.106, f32[]{:T(128)} %constant.74.clone.1), padding=0_0x0_0x0_0x0_0x1_7 | pad | bytes 2433028 | tf_op jit(solution)/shard_map/broadcast_in_dim | solution.py:32
  29.4 0.0 copy-start.7
  29.4 0.0 copy-start.8
  29.4 0.2 copy.71
  29.6 0.9 copy-done.7
  30.6 0.0 copy-done.8
  30.6 15.9 %fusion.22 = f32[4,4,8,17,64]{4,2,3,1,0:T(8,128)S(1)} fusion(f32[3,3,3,64,64]{4,3,2,1,0:T(8,128)S(1)} %copy-done.7, f32[64,6,6,1,7,2]{0,4,5,2,1,3:T(8,128)S(1)} %slice.107, f32[64,6,6,1,8,17]{0,4,5,2,1,3:T(8,128)S(1)} %copy.71, pred[8,17]{0,1:T(8,128)(4,1)S(1)} %copy-done.8), kind=kOutput, calls=%fused_computation.21 | convolution fusion | flops 2898020352 | bytes 2381960 | tf_op jit(solution)/shard_map/conv_general_dilated | solution.py:31
  46.4 0.3 copy.72
  46.7 0.1 slice.108
  46.8 0.0 copy-start.4
  46.8 0.6 copy.75
  47.5 0.3 copy-done.4
  47.8 1.0 fusion.24
  48.8 3.9 %collective-permute-start.4 = (f32[128,1,2,64]{0,3,2,1:T(8,128)S(1)}, f32[128,1,2,64]{0,3,2,1:T(8,128)S(1)}, u32[]{:S(2)}, u32[]{:S(2)}) collective-permute-start(f32[128,1,2,64]{0,3,2,1:T(8,128)S(1)} %get-tuple-element.53), channel_id=1, source_target_pairs={{0,4},{4,8},{8,12},{12,16},{16,20},{20,24},{24,28},{1,5},{5,9},{9,... | collective-permute-start | bytes 196616 | tf_op jit(solution)/shard_map/ppermute | solution.py:15
  52.8 1.9 %collective-permute-start.5 = (f32[128,1,2,64]{0,3,2,1:T(8,128)S(1)}, f32[128,1,2,64]{0,3,2,1:T(8,128)S(1)}, u32[]{:S(2)}, u32[]{:S(2)}) collective-permute-start(f32[128,1,2,64]{0,3,2,1:T(8,128)S(1)} %get-tuple-element.54), channel_id=1, source_target_pairs={{4,0},{8,4},{12,8},{16,12},{20,16},{24,20},{28,24},{5,1},{9,5},{13... | collective-permute-start | bytes 196616 | tf_op jit(solution)/shard_map/ppermute | solution.py:17
  54.7 0.0 collective-permute-done.4
  54.7 3.6 %collective-permute-done.5 = f32[128,1,2,64]{0,3,2,1:T(8,128)S(1)} collective-permute-done((f32[128,1,2,64]{0,3,2,1:T(8,128)S(1)}, f32[128,1,2,64]{0,3,2,1:T(8,128)S(1)}, u32[]{:S(2)}, u32[]{:S(2)}) %collective-permute-start.5) | collective-permute-done | bytes 65568 | tf_op jit(solution)/shard_map/ppermute | solution.py:17
  58.4 3.2 %collective-permute-start.6 = (f32[128,4,1,64]{0,3,2,1:T(8,128)S(1)}, f32[128,4,1,64]{0,3,2,1:T(8,128)S(1)}, u32[]{:S(2)}, u32[]{:S(2)}) collective-permute-start(f32[128,4,1,64]{0,3,2,1:T(8,128)S(1)} %get-tuple-element.49), channel_id=1, source_target_pairs={{0,1},{1,2},{2,3},{4,5},{5,6},{6,7},{8,9},{9,10},{10,11},{12,13},{... | collective-permute-start | bytes 393224 | tf_op jit(solution)/shard_map/ppermute | solution.py:15
  61.6 1.5 %collective-permute-start.7 = (f32[128,4,1,64]{0,3,2,1:T(8,128)S(1)}, f32[128,4,1,64]{0,3,2,1:T(8,128)S(1)}, u32[]{:S(2)}, u32[]{:S(2)}) collective-permute-start(f32[128,4,1,64]{0,3,2,1:T(8,128)S(1)} %get-tuple-element.50), channel_id=1, source_target_pairs={{1,0},{2,1},{3,2},{5,4},{6,5},{7,6},{9,8},{10,9},{11,10},{13,12},{... | collective-permute-start | bytes 393224 | tf_op jit(solution)/shard_map/ppermute | solution.py:17
  63.1 0.4 collective-permute-done.6
  63.5 3.8 %collective-permute-done.7 = f32[128,4,1,64]{0,3,2,1:T(8,128)S(1)} collective-permute-done((f32[128,4,1,64]{0,3,2,1:T(8,128)S(1)}, f32[128,4,1,64]{0,3,2,1:T(8,128)S(1)}, u32[]{:S(2)}, u32[]{:S(2)}) %collective-permute-start.7) | collective-permute-done | bytes 131104 | tf_op jit(solution)/shard_map/ppermute | solution.py:17
  67.4 0.3 copy.107
  67.7 0.0 copy-start.6
  67.7 0.1 pad.9.clone
  67.9 0.0 copy-done
  67.9 0.5 copy-done.6
  68.4 3.3 %negate_multiply_fusion.1 = (f32[2,2,8,9,128]{4,2,3,1,0:T(8,128)S(1)}, f32[2,2,8,9,128]{4,2,3,1,0:T(8,128)S(1)}) fusion(f32[3,3,3,128,128]{4,3,2,1,0:T(8,128)S(1)} %copy-done, f32[128,4,4,1,7,2]{0,4,5,2,1,3:T(8,128)S(1)} %slice.114, f32[128,4,4,1,8,9]{0,4,5,2,1,3:T(8,128)S(1)} %copy.79, pred[8,9]{0,1:T(8,128)(4,1)S(1)} %copy-done.6), kind=kOutput, calls=%fused_computation.66 | convolution fusion | flops 1529511936 | bytes 2768968 | tf_op jit(solution)/shard_map/conv_general_dilated | solution.py:31
  71.7 0.1 copy.82
  71.8 0.1 copy.80
  71.9 0.3 fusion.55
  72.2 0.0 copy-start.3
  72.2 14.4 %all_gather.6 = f32[128,2,8,64]{0,3,1,2:T(8,128)S(1)} all-gather(f32[128,2,2,64]{0,3,1,2:T(8,128)S(1)} %copy.84), channel_id=1, replica_groups=mesh['slab'=8,'grp'=4] {'grp'}, dimensions={2}, use_global_device_ids=true | all-gather | bytes 655360 | tf_op jit(solution)/shard_map/all_gather | solution.py:49
  86.6 0.1 copy.87
  86.8 0.0 copy-done.3
  86.8 0.6 fusion.43
  87.4 0.0 copy-start.5
  87.4 0.1 copy.89
  87.5 12.7 %all-gather = f32[1,256,1,4,32]{4,3,2,0,1:T(4,128)S(1)} all-gather(f32[1,64,1,4,32]{4,3,2,0,1:T(4,128)S(1)} %copy.89), channel_id=2, replica_groups=mesh['slab'=8,'grp'=4] {'grp'}, dimensions={1}, use_global_device_ids=true | all-gather | bytes 163840 | tf_op jit(solution)/shard_map/all_gather | solution.py:51
  100.2 0.2 copy.108
  100.5 0.0 copy-done.5
  100.5 0.0 copy-start.1
  100.5 2.7 %fusion.14 = f32[1,4,8,5,128]{4,2,3,1,0:T(8,128)S(1)} fusion(f32[3,3,3,256,128]{4,3,2,1,0:T(8,128)} %param.19, f32[256,1,4,1,7,2]{0,4,5,2,3,1:T(8,128)S(1)} %slice.118, f32[256,1,4,1,8,5]{0,4,5,2,3,1:T(8,128)S(1)} %copy.92, pred[8,5]{0,1:T(8,128)(4,1)S(1)} %copy-done.5), kind=kOutput, calls=%fused_computation.16 | convolution fusion | flops 472051712 | bytes 1482792 | tf_op jit(solution)/shard_map/conv_general_dilated | solution.py:31
  103.3 2.6 %fusion.17 = f32[1,4,8,5,128]{4,2,3,1,0:T(8,128)S(1)} fusion(f32[3,3,3,256,128]{4,3,2,1,0:T(8,128)} %param.19, f32[256,1,4,1,7,2]{0,4,5,2,3,1:T(8,128)S(1)} %slice.118, f32[256,1,4,1,8,5]{0,4,5,2,3,1:T(8,128)S(1)} %copy.92, pred[8,5]{0,1:T(8,128)(4,1)S(1)} %copy-done.5), kind=kOutput, calls=%fused_computation.17 | convolution fusion | flops 472051712 | bytes 1482792 | tf_op jit(solution)/shard_map/conv_general_dilated | solution.py:31
  105.9 8.8 %collective-permute-start.8 = (f32[128,1,4,32]{0,2,3,1:T(4,128)S(1)}, f32[128,1,4,32]{0,2,3,1:T(4,128)S(1)}, u32[]{:S(2)}, u32[]{:S(2)}) collective-permute-start(f32[128,1,4,32]{0,2,3,1:T(4,128)S(1)} %slice_bitcast_fusion.1), channel_id=1, source_target_pairs={{0,4},{4,8},{8,12},{12,16},{16,20},{20,24},{24,28},{1,5},{5,9},{9,... | collective-permute-start | bytes 196616 | tf_op jit(solution)/shard_map/ppermute | solution.py:27
  114.7 2.2 %collective-permute-start.9 = (f32[128,1,4,32]{0,2,3,1:T(4,128)S(1)}, f32[128,1,4,32]{0,2,3,1:T(4,128)S(1)}, u32[]{:S(2)}, u32[]{:S(2)}) collective-permute-start(f32[128,1,4,32]{0,2,3,1:T(4,128)S(1)} %slice_bitcast_fusion), channel_id=1, source_target_pairs={{4,0},{8,4},{12,8},{16,12},{20,16},{24,20},{28,24},{5,1},{9,5},{13... | collective-permute-start | bytes 196616 | tf_op jit(solution)/shard_map/ppermute | solution.py:27
  116.9 3.6 %convolution_select_fusion.1 = f32[1,4,8,5,128]{4,2,3,1,0:T(8,128)S(1)} fusion(f32[3,3,3,256,128]{4,3,2,1,0:T(8,128)S(1)} %copy-done.1, f32[256,1,4,1,7,2]{0,4,5,2,3,1:T(8,128)S(1)} %slice.118, f32[256,1,4,1,8,5]{0,4,5,2,3,1:T(8,128)S(1)} %copy.92, pred[8,5]{0,1:T(8,128)(4,1)S(1)} %copy-done.5), kind=kOutput, calls=%fused_computation.18 | convolution fusion | flops 472051712 | bytes 3842088 | tf_op jit(solution)/shard_map/conv_general_dilated | solution.py:31
  120.6 0.0 collective-permute-done.8
  120.6 0.0 collective-permute-done.9
  120.6 0.3 fusion.67
  120.9 0.7 copy.99
  (30 shorter events, 0.5 us)
Async XLA Ops:
  0.0 67.9 %copy-start = (f32[3,3,3,128,128]{4,3,2,1,0:T(8,128)S(1)}, f32[3,3,3,128,128]{4,3,2,1,0:T(8,128)}, u32[]{:S(2)}) copy-start(f32[3,3,3,128,128]{4,3,2,1,0:T(8,128)} %param.17) | copy-start | bytes 5308420
  0.0 7.6 %copy-start.2 = (f32[64,4,4,128]{3,2,1,0:T(4,128)S(1)}, f32[64,4,4,128]{3,2,1,0:T(4,128)}, u32[]{:S(2)}) copy-start(f32[64,4,4,128]{3,2,1,0:T(4,128)} %param.14) | copy-start | bytes 1572868
  1.2 6.5 %collective-permute-start = (f32[64,1,4,128]{3,0,2,1:T(8,128)S(1)}, f32[64,1,4,128]{3,0,2,1:T(8,128)S(1)}, u32[]{:S(2)}, u32[]{:S(2)}) collective-permute-start(f32[64,1,4,128]{3,0,2,1:T(8,128)S(1)} %copy.117), channel_id=1, source_target_pairs={{0,4},{4,8},{8,12},{12,16},{16,20},{20,24},{24,28},{1,5},{5,9},{9,... | collective-permute-start | bytes 393224 | tf_op jit(solution)/shard_map/ppermute | solution.py:15
  5.7 6.3 %collective-permute-start.1 = (f32[64,1,4,128]{3,0,2,1:T(8,128)S(1)}, f32[64,1,4,128]{3,0,2,1:T(8,128)S(1)}, u32[]{:S(2)}, u32[]{:S(2)}) collective-permute-start(f32[64,1,4,128]{3,0,2,1:T(8,128)S(1)} %copy.118), channel_id=1, source_target_pairs={{4,0},{8,4},{12,8},{16,12},{20,16},{24,20},{28,24},{5,1},{9,5},{13... | collective-permute-start | bytes 393224 | tf_op jit(solution)/shard_map/ppermute | solution.py:17
  12.0 5.8 %collective-permute-start.2 = (f32[64,6,1,128]{3,0,2,1:T(8,128)S(1)}, f32[64,6,1,128]{3,0,2,1:T(8,128)S(1)}, u32[]{:S(2)}, u32[]{:S(2)}) collective-permute-start(f32[64,6,1,128]{3,0,2,1:T(8,128)S(1)} %get-tuple-element.45), channel_id=1, source_target_pairs={{0,1},{1,2},{2,3},{4,5},{5,6},{6,7},{8,9},{9,10},{10,11},{12,13},{... | collective-permute-start | bytes 589832 | tf_op jit(solution)/shard_map/ppermute | solution.py:15
  15.2 6.4 %collective-permute-start.3 = (f32[64,6,1,128]{3,0,2,1:T(8,128)S(1)}, f32[64,6,1,128]{3,0,2,1:T(8,128)S(1)}, u32[]{:S(2)}, u32[]{:S(2)}) collective-permute-start(f32[64,6,1,128]{3,0,2,1:T(8,128)S(1)} %get-tuple-element.46), channel_id=1, source_target_pairs={{1,0},{2,1},{3,2},{5,4},{6,5},{7,6},{9,8},{10,9},{11,10},{13,12},{... | collective-permute-start | bytes 589832 | tf_op jit(solution)/shard_map/ppermute | solution.py:17
  29.4 1.2 copy-start.7
  29.4 1.2 copy-start.8
  46.8 1.0 copy-start.4
  48.8 5.9 %collective-permute-start.4 = (f32[128,1,2,64]{0,3,2,1:T(8,128)S(1)}, f32[128,1,2,64]{0,3,2,1:T(8,128)S(1)}, u32[]{:S(2)}, u32[]{:S(2)}) collective-permute-start(f32[128,1,2,64]{0,3,2,1:T(8,128)S(1)} %get-tuple-element.53), channel_id=1, source_target_pairs={{0,4},{4,8},{8,12},{12,16},{16,20},{20,24},{24,28},{1,5},{5,9},{9,... | collective-permute-start | bytes 196616 | tf_op jit(solution)/shard_map/ppermute | solution.py:15
  52.8 5.6 %collective-permute-start.5 = (f32[128,1,2,64]{0,3,2,1:T(8,128)S(1)}, f32[128,1,2,64]{0,3,2,1:T(8,128)S(1)}, u32[]{:S(2)}, u32[]{:S(2)}) collective-permute-start(f32[128,1,2,64]{0,3,2,1:T(8,128)S(1)} %get-tuple-element.54), channel_id=1, source_target_pairs={{4,0},{8,4},{12,8},{16,12},{20,16},{24,20},{28,24},{5,1},{9,5},{13... | collective-permute-start | bytes 196616 | tf_op jit(solution)/shard_map/ppermute | solution.py:17
  58.4 5.1 %collective-permute-start.6 = (f32[128,4,1,64]{0,3,2,1:T(8,128)S(1)}, f32[128,4,1,64]{0,3,2,1:T(8,128)S(1)}, u32[]{:S(2)}, u32[]{:S(2)}) collective-permute-start(f32[128,4,1,64]{0,3,2,1:T(8,128)S(1)} %get-tuple-element.49), channel_id=1, source_target_pairs={{0,1},{1,2},{2,3},{4,5},{5,6},{6,7},{8,9},{9,10},{10,11},{12,13},{... | collective-permute-start | bytes 393224 | tf_op jit(solution)/shard_map/ppermute | solution.py:15
  61.6 5.7 %collective-permute-start.7 = (f32[128,4,1,64]{0,3,2,1:T(8,128)S(1)}, f32[128,4,1,64]{0,3,2,1:T(8,128)S(1)}, u32[]{:S(2)}, u32[]{:S(2)}) collective-permute-start(f32[128,4,1,64]{0,3,2,1:T(8,128)S(1)} %get-tuple-element.50), channel_id=1, source_target_pairs={{1,0},{2,1},{3,2},{5,4},{6,5},{7,6},{9,8},{10,9},{11,10},{13,12},{... | collective-permute-start | bytes 393224 | tf_op jit(solution)/shard_map/ppermute | solution.py:17
  67.7 0.7 copy-start.6
  72.2 14.6 %copy-start.3 = (f32[2,2,2,128,64]{3,4,2,1,0:T(8,128)S(1)}, f32[2,2,2,128,64]{3,4,2,1,0:T(8,128)}, u32[]{:S(2)}) copy-start(f32[2,2,2,128,64]{3,4,2,1,0:T(8,128)} %param.18) | copy-start | bytes 786436
  87.4 13.2 %copy-start.5 = (pred[8,5]{0,1:T(8,128)(4,1)S(1)}, pred[8,5]{0,1:T(8,128)(4,1)}, u32[]{:S(2)}) copy-start(pred[8,5]{0,1:T(8,128)(4,1)} %constant.213) | copy-start | bytes 124
  100.5 16.4 %copy-start.1 = (f32[3,3,3,256,128]{4,3,2,1,0:T(8,128)S(1)}, f32[3,3,3,256,128]{4,3,2,1,0:T(8,128)}, u32[]{:S(2)}) copy-start(f32[3,3,3,256,128]{4,3,2,1,0:T(8,128)} %param.19) | copy-start | bytes 10616836
  105.9 14.7 %collective-permute-start.8 = (f32[128,1,4,32]{0,2,3,1:T(4,128)S(1)}, f32[128,1,4,32]{0,2,3,1:T(4,128)S(1)}, u32[]{:S(2)}, u32[]{:S(2)}) collective-permute-start(f32[128,1,4,32]{0,2,3,1:T(4,128)S(1)} %slice_bitcast_fusion.1), channel_id=1, source_target_pairs={{0,4},{4,8},{8,12},{12,16},{16,20},{20,24},{24,28},{1,5},{5,9},{9,... | collective-permute-start | bytes 196616 | tf_op jit(solution)/shard_map/ppermute | solution.py:27
  114.7 5.8 %collective-permute-start.9 = (f32[128,1,4,32]{0,2,3,1:T(4,128)S(1)}, f32[128,1,4,32]{0,2,3,1:T(4,128)S(1)}, u32[]{:S(2)}, u32[]{:S(2)}) collective-permute-start(f32[128,1,4,32]{0,2,3,1:T(4,128)S(1)} %slice_bitcast_fusion), channel_id=1, source_target_pairs={{4,0},{8,4},{12,8},{16,12},{20,16},{24,20},{28,24},{5,1},{9,5},{13... | collective-permute-start | bytes 196616 | tf_op jit(solution)/shard_map/ppermute | solution.py:27
where the time goes:
time: 123 us; the launch traced here: 122 us
  starting transfers between devices  32.4 us (26%)
  matrix products  29.6 us (24%)
  blocking collectives  27.2 us (22%)
  waiting for transfers between devices  17.1 us (14%)
  local copies, waits for them, and re-layouts  14 us (11%)
    conv_general_dilated x7, matrix products, convolve(): lax.conv_general_dilated(field[None], kernel, (stride, stride, stride), p...  29.6 us
    ppermute x4, waiting for transfers between devices, padded_2(): lax.ppermute(head, axis, [((i + 1) % count, i) for i in range(ends)])  15.4 us
    ppermute x4, starting transfers between devices, padded_2(): lax.ppermute(tail, axis, [(i, (i + 1) % count) for i in range(ends)])  14.8 us
    all_gather x1, blocking collectives, per_device(): gathered = lax.all_gather(level_two, 'grp', axis=2, tiled=True)  14.4 us
    all_gather x1, blocking collectives, per_device(): coarse = lax.all_gather(shares, 'grp', axis=0, tiled=True)  12.7 us
    ppermute x2, starting transfers between devices, from_behind(): return lax.ppermute(shard, axis, pairs)  11 us
    unnamed x25, local copies, waits for them, and re-layouts  6.75 us
    ppermute x4, starting transfers between devices, padded_2(): lax.ppermute(head, axis, [((i + 1) % count, i) for i in range(ends)])  6.65 us
  transfers between devices with their start and end apart: 10, of which 6 were waited for; matrix products, arithmetic and copies ran while one was open for 3% of the time, Pallas kernels for 0%

commit v1 on v0

--- a/solution.py
+++ b/solution.py
@@ -34,7 +34,7 @@
         (stride, stride, stride),
         padding,
         dimension_numbers=("NCDHW", "DHWIO", "NCDHW"),
-        precision=lax.Precision.HIGHEST,
+        precision=lax.Precision.HIGH,
     )[0]
 
 

time: 123 us -> 112 us (0.911)
  matrix products: 29.6 us -> 17.7 us
  waiting for transfers between devices: 17.1 us -> 19 us
    conv_general_dilated x7, matrix products: 29.6 us -> 17.7 us  [convolve(): lax.conv_general_dilated(field[None], kernel, (stride, stride, stride), p...]
    ppermute x2, waiting for transfers between devices: 0.01 us -> 1.62 us  [from_behind(): return lax.ppermute(shard, axis, pairs)]
  transfers between devices with their start and end apart: 10 -> 10, of which waited for: 6 -> 7; matrix products, arithmetic and copies ran while one was open for 3% -> 2% of each run, Pallas kernels for 0% -> 0%
where the time goes in v1:
time: 112 us; the launch traced here: 111 us
  starting transfers between devices  32 us (29%)
  blocking collectives  27.2 us (24%)
  waiting for transfers between devices  19 us (17%)
  matrix products  17.7 us (16%)
  local copies, waits for them, and re-layouts  14 us (12%)
    conv_general_dilated x7, matrix products, convolve(): lax.conv_general_dilated(field[None], kernel, (stride, stride, stride), p...  17.7 us
    ppermute x4, waiting for transfers between devices, padded_2(): lax.ppermute(head, axis, [((i + 1) % count, i) for i in range(ends)])  15.4 us
    ppermute x4, starting transfers between devices, padded_2(): lax.ppermute(tail, axis, [(i, (i + 1) % count) for i in range(ends)])  14.8 us
    all_gather x1, blocking collectives, per_device(): gathered = lax.all_gather(level_two, 'grp', axis=2, tiled=True)  14.4 us
    all_gather x1, blocking collectives, per_device(): coarse = lax.all_gather(shares, 'grp', axis=0, tiled=True)  12.7 us
    ppermute x2, starting transfers between devices, from_behind(): return lax.ppermute(shard, axis, pairs)  10.7 us
    unnamed x25, local copies, waits for them, and re-layouts  6.57 us
    ppermute x4, starting transfers between devices, padded_2(): lax.ppermute(head, axis, [((i + 1) % count, i) for i in range(ends)])  6.43 us
  transfers between devices with their start and end apart: 10, of which 7 were waited for; matrix products, arithmetic and copies ran while one was open for 2% of the time, Pallas kernels for 0%

profile of v1, /device:TPU:1, one launch (start us, length us, event | category | flops | bytes accessed | tf_op | source)
XLA Modules:
  0.0 111.1 jit_solution(5088710529204012672)
XLA Ops:
  0.0 0.0 copy-start
  0.0 1.1 %fusion.97 = (f32[64,1,4,128]{3,2,1,0:T(4,128)S(1)}, f32[64,1,4,128]{3,2,1,0:T(4,128)S(1)}) fusion(f32[64,4,4,128]{3,2,1,0:T(4,128)} %param.14), kind=kLoop, calls=%fused_computation.132 | loop fusion | bytes 524288 | tf_op jit(solution)/shard_map/slice | solution.py:11
  1.2 4.5 %collective-permute-start = (f32[64,1,4,128]{3,0,2,1:T(8,128)S(1)}, f32[64,1,4,128]{3,0,2,1:T(8,128)S(1)}, u32[]{:S(2)}, u32[]{:S(2)}) collective-permute-start(f32[64,1,4,128]{3,0,2,1:T(8,128)S(1)} %copy.117), channel_id=1, source_target_pairs={{0,4},{4,8},{8,12},{12,16},{16,20},{20,24},{24,28},{1,5},{5,9},{9,... | collective-permute-start | bytes 393224 | tf_op jit(solution)/shard_map/ppermute | solution.py:15
  5.7 1.9 %collective-permute-start.1 = (f32[64,1,4,128]{3,0,2,1:T(8,128)S(1)}, f32[64,1,4,128]{3,0,2,1:T(8,128)S(1)}, u32[]{:S(2)}, u32[]{:S(2)}) collective-permute-start(f32[64,1,4,128]{3,0,2,1:T(8,128)S(1)} %copy.118), channel_id=1, source_target_pairs={{4,0},{8,4},{12,8},{16,12},{20,16},{24,20},{28,24},{5,1},{9,5},{13... | collective-permute-start | bytes 393224 | tf_op jit(solution)/shard_map/ppermute | solution.py:17
  7.6 0.0 collective-permute-done
  7.6 0.0 copy-done.2
  7.7 0.2 constant_dynamic-update-slice_fusion.1
  7.8 4.2 %collective-permute-done.1 = f32[64,1,4,128]{3,0,2,1:T(8,128)S(1)} collective-permute-done((f32[64,1,4,128]{3,0,2,1:T(8,128)S(1)}, f32[64,1,4,128]{3,0,2,1:T(8,128)S(1)}, u32[]{:S(2)}, u32[]{:S(2)}) %collective-permute-start.1) | collective-permute-done | bytes 131104 | tf_op jit(solution)/shard_map/ppermute | solution.py:17
  12.0 3.2 %collective-permute-start.2 = (f32[64,6,1,128]{3,0,2,1:T(8,128)S(1)}, f32[64,6,1,128]{3,0,2,1:T(8,128)S(1)}, u32[]{:S(2)}, u32[]{:S(2)}) collective-permute-start(f32[64,6,1,128]{3,0,2,1:T(8,128)S(1)} %get-tuple-element.45), channel_id=1, source_target_pairs={{0,1},{1,2},{2,3},{4,5},{5,6},{6,7},{8,9},{9,10},{10,11},{12,13},{... | collective-permute-start | bytes 589832 | tf_op jit(solution)/shard_map/ppermute | solution.py:15
  15.2 1.3 %collective-permute-start.3 = (f32[64,6,1,128]{3,0,2,1:T(8,128)S(1)}, f32[64,6,1,128]{3,0,2,1:T(8,128)S(1)}, u32[]{:S(2)}, u32[]{:S(2)}) collective-permute-start(f32[64,6,1,128]{3,0,2,1:T(8,128)S(1)} %get-tuple-element.46), channel_id=1, source_target_pairs={{1,0},{2,1},{3,2},{5,4},{6,5},{7,6},{9,8},{10,9},{11,10},{13,12},{... | collective-permute-start | bytes 589832 | tf_op jit(solution)/shard_map/ppermute | solution.py:17
  16.5 1.3 %collective-permute-done.2 = f32[64,6,1,128]{3,0,2,1:T(8,128)S(1)} collective-permute-done((f32[64,6,1,128]{3,0,2,1:T(8,128)S(1)}, f32[64,6,1,128]{3,0,2,1:T(8,128)S(1)}, u32[]{:S(2)}, u32[]{:S(2)}) %collective-permute-start.2) | collective-permute-done | bytes 196640 | tf_op jit(solution)/shard_map/ppermute | solution.py:15
  17.8 3.8 %collective-permute-done.3 = f32[64,6,1,128]{3,0,2,1:T(8,128)S(1)} collective-permute-done((f32[64,6,1,128]{3,0,2,1:T(8,128)S(1)}, f32[64,6,1,128]{3,0,2,1:T(8,128)S(1)}, u32[]{:S(2)}, u32[]{:S(2)}) %collective-permute-start.3) | collective-permute-done | bytes 196640 | tf_op jit(solution)/shard_map/ppermute | solution.py:17
  21.7 0.1 maximum_bitcast_fusion
  21.8 4.2 %copy.106 = f32[64,6,6,1,128]{0,3,4,2,1:T(1,128)} copy(f32[64,6,6,1,128]{4,0,2,1,3:T(8,128)S(1)} %maximum_bitcast_fusion) | data formatting | bytes 2359296
  26.0 3.4 %pad.6.clone = f32[64,6,6,1,136]{0,3,4,2,1:T(1,128)S(1)} pad(f32[64,6,6,1,128]{0,3,4,2,1:T(1,128)} %copy.106, f32[]{:T(128)} %constant.74.clone.1), padding=0_0x0_0x0_0x0_0x1_7 | pad | bytes 2433028 | tf_op jit(solution)/shard_map/broadcast_in_dim | solution.py:32
  29.4 0.0 copy-start.7
  29.4 0.0 copy-start.8
  29.4 0.2 copy.71
  29.6 0.9 copy-done.7
  30.6 0.0 copy-done.8
  30.6 8.9 %fusion.22 = f32[4,4,8,17,64]{4,2,3,1,0:T(8,128)S(1)} fusion(f32[3,3,3,64,64]{4,3,2,1,0:T(8,128)S(1)} %copy-done.7, f32[64,6,6,1,7,2]{0,4,5,2,1,3:T(8,128)S(1)} %slice.107, f32[64,6,6,1,8,17]{0,4,5,2,1,3:T(8,128)S(1)} %copy.71, pred[8,17]{0,1:T(8,128)(4,1)S(1)} %copy-done.8), kind=kOutput, calls=%fused_computation.21 | convolution fusion | flops 1454131200 | bytes 2381960 | tf_op jit(solution)/shard_map/conv_general_dilated | solution.py:31
  39.4 0.3 copy.72
  39.7 0.1 slice.108
  39.8 0.0 copy-start.4
  39.8 0.8 copy.75
  40.6 0.1 copy-done.4
  40.8 0.6 fusion.24
  41.4 3.9 %collective-permute-start.4 = (f32[128,1,2,64]{0,3,2,1:T(8,128)S(1)}, f32[128,1,2,64]{0,3,2,1:T(8,128)S(1)}, u32[]{:S(2)}, u32[]{:S(2)}) collective-permute-start(f32[128,1,2,64]{0,3,2,1:T(8,128)S(1)} %get-tuple-element.53), channel_id=1, source_target_pairs={{0,4},{4,8},{8,12},{12,16},{16,20},{20,24},{24,28},{1,5},{5,9},{9,... | collective-permute-start | bytes 196616 | tf_op jit(solution)/shard_map/ppermute | solution.py:15
  45.4 1.9 %collective-permute-start.5 = (f32[128,1,2,64]{0,3,2,1:T(8,128)S(1)}, f32[128,1,2,64]{0,3,2,1:T(8,128)S(1)}, u32[]{:S(2)}, u32[]{:S(2)}) collective-permute-start(f32[128,1,2,64]{0,3,2,1:T(8,128)S(1)} %get-tuple-element.54), channel_id=1, source_target_pairs={{4,0},{8,4},{12,8},{16,12},{20,16},{24,20},{28,24},{5,1},{9,5},{13... | collective-permute-start | bytes 196616 | tf_op jit(solution)/shard_map/ppermute | solution.py:17
  47.3 0.0 collective-permute-done.4
  47.3 3.6 %collective-permute-done.5 = f32[128,1,2,64]{0,3,2,1:T(8,128)S(1)} collective-permute-done((f32[128,1,2,64]{0,3,2,1:T(8,128)S(1)}, f32[128,1,2,64]{0,3,2,1:T(8,128)S(1)}, u32[]{:S(2)}, u32[]{:S(2)}) %collective-permute-start.5) | collective-permute-done | bytes 65568 | tf_op jit(solution)/shard_map/ppermute | solution.py:17
  51.0 3.2 %collective-permute-start.6 = (f32[128,4,1,64]{0,3,2,1:T(8,128)S(1)}, f32[128,4,1,64]{0,3,2,1:T(8,128)S(1)}, u32[]{:S(2)}, u32[]{:S(2)}) collective-permute-start(f32[128,4,1,64]{0,3,2,1:T(8,128)S(1)} %get-tuple-element.49), channel_id=1, source_target_pairs={{0,1},{1,2},{2,3},{4,5},{5,6},{6,7},{8,9},{9,10},{10,11},{12,13},{... | collective-permute-start | bytes 393224 | tf_op jit(solution)/shard_map/ppermute | solution.py:15
  54.2 1.3 %collective-permute-start.7 = (f32[128,4,1,64]{0,3,2,1:T(8,128)S(1)}, f32[128,4,1,64]{0,3,2,1:T(8,128)S(1)}, u32[]{:S(2)}, u32[]{:S(2)}) collective-permute-start(f32[128,4,1,64]{0,3,2,1:T(8,128)S(1)} %get-tuple-element.50), channel_id=1, source_target_pairs={{1,0},{2,1},{3,2},{5,4},{6,5},{7,6},{9,8},{10,9},{11,10},{13,12},{... | collective-permute-start | bytes 393224 | tf_op jit(solution)/shard_map/ppermute | solution.py:17
  55.5 0.6 collective-permute-done.6
  56.1 3.8 %collective-permute-done.7 = f32[128,4,1,64]{0,3,2,1:T(8,128)S(1)} collective-permute-done((f32[128,4,1,64]{0,3,2,1:T(8,128)S(1)}, f32[128,4,1,64]{0,3,2,1:T(8,128)S(1)}, u32[]{:S(2)}, u32[]{:S(2)}) %collective-permute-start.7) | collective-permute-done | bytes 131104 | tf_op jit(solution)/shard_map/ppermute | solution.py:17
  60.0 0.3 copy.107
  60.3 0.0 copy-start.6
  60.3 0.1 pad.9.clone
  60.5 0.0 copy-done
  60.5 0.5 copy-done.6
  61.0 1.7 %negate_multiply_fusion.1 = (f32[2,2,8,9,128]{4,2,3,1,0:T(8,128)S(1)}, f32[2,2,8,9,128]{4,2,3,1,0:T(8,128)S(1)}) fusion(f32[3,3,3,128,128]{4,3,2,1,0:T(8,128)S(1)} %copy-done, f32[128,4,4,1,7,2]{0,4,5,2,1,3:T(8,128)S(1)} %slice.114, f32[128,4,4,1,8,9]{0,4,5,2,1,3:T(8,128)S(1)} %copy.79, pred[8,9]{0,1:T(8,128)(4,1)S(1)} %copy-done.6), kind=kOutput, calls=%fused_computation.66 | convolution fusion | flops 765100032 | bytes 2768968 | tf_op jit(solution)/shard_map/conv_general_dilated | solution.py:31
  62.7 0.1 copy.82
  62.8 0.1 copy.80
  62.9 0.3 fusion.55
  63.2 0.0 copy-start.3
  63.2 14.4 %all_gather.6 = f32[128,2,8,64]{0,3,1,2:T(8,128)S(1)} all-gather(f32[128,2,2,64]{0,3,1,2:T(8,128)S(1)} %copy.84), channel_id=1, replica_groups=mesh['slab'=8,'grp'=4] {'grp'}, dimensions={2}, use_global_device_ids=true | all-gather | bytes 655360 | tf_op jit(solution)/shard_map/all_gather | solution.py:49
  77.7 0.1 copy.87
  77.8 0.4 fusion.43
  78.2 0.0 copy-start.5
  78.2 0.1 copy.89
  78.3 12.7 %all-gather = f32[1,256,1,4,32]{4,3,2,0,1:T(4,128)S(1)} all-gather(f32[1,64,1,4,32]{4,3,2,0,1:T(4,128)S(1)} %copy.89), channel_id=2, replica_groups=mesh['slab'=8,'grp'=4] {'grp'}, dimensions={1}, use_global_device_ids=true | all-gather | bytes 163840 | tf_op jit(solution)/shard_map/all_gather | solution.py:51
  91.0 0.2 copy.108
  91.3 0.0 copy-done.5
  91.3 0.0 copy-start.1
  91.4 2.2 %fusion.14 = f32[1,4,8,5,128]{4,2,3,1,0:T(8,128)S(1)} fusion(f32[3,3,3,256,128]{4,3,2,1,0:T(8,128)} %param.19, f32[256,1,4,1,7,2]{0,4,5,2,3,1:T(8,128)S(1)} %slice.118, f32[256,1,4,1,8,5]{0,4,5,2,3,1:T(8,128)S(1)} %copy.92, pred[8,5]{0,1:T(8,128)(4,1)S(1)} %copy-done.5), kind=kOutput, calls=%fused_computation.16 | convolution fusion | flops 236122112 | bytes 1482792 | tf_op jit(solution)/shard_map/conv_general_dilated | solution.py:31
  93.5 2.0 %fusion.17 = f32[1,4,8,5,128]{4,2,3,1,0:T(8,128)S(1)} fusion(f32[3,3,3,256,128]{4,3,2,1,0:T(8,128)} %param.19, f32[256,1,4,1,7,2]{0,4,5,2,3,1:T(8,128)S(1)} %slice.118, f32[256,1,4,1,8,5]{0,4,5,2,3,1:T(8,128)S(1)} %copy.92, pred[8,5]{0,1:T(8,128)(4,1)S(1)} %copy-done.5), kind=kOutput, calls=%fused_computation.17 | convolution fusion | flops 236122112 | bytes 1482792 | tf_op jit(solution)/shard_map/conv_general_dilated | solution.py:31
  95.6 8.8 %collective-permute-start.8 = (f32[128,1,4,32]{0,2,3,1:T(4,128)S(1)}, f32[128,1,4,32]{0,2,3,1:T(4,128)S(1)}, u32[]{:S(2)}, u32[]{:S(2)}) collective-permute-start(f32[128,1,4,32]{0,2,3,1:T(4,128)S(1)} %slice_bitcast_fusion.1), channel_id=1, source_target_pairs={{0,4},{4,8},{8,12},{12,16},{16,20},{20,24},{24,28},{1,5},{5,9},{9,... | collective-permute-start | bytes 196616 | tf_op jit(solution)/shard_map/ppermute | solution.py:27
  104.4 1.9 %collective-permute-start.9 = (f32[128,1,4,32]{0,2,3,1:T(4,128)S(1)}, f32[128,1,4,32]{0,2,3,1:T(4,128)S(1)}, u32[]{:S(2)}, u32[]{:S(2)}) collective-permute-start(f32[128,1,4,32]{0,2,3,1:T(4,128)S(1)} %slice_bitcast_fusion), channel_id=1, source_target_pairs={{4,0},{8,4},{12,8},{16,12},{20,16},{24,20},{28,24},{5,1},{9,5},{13... | collective-permute-start | bytes 196616 | tf_op jit(solution)/shard_map/ppermute | solution.py:27
  106.4 0.0 copy-done.1
  106.4 2.0 %convolution_select_fusion.1 = f32[1,4,8,5,128]{4,2,3,1,0:T(8,128)S(1)} fusion(f32[3,3,3,256,128]{4,3,2,1,0:T(8,128)S(1)} %copy-done.1, f32[256,1,4,1,7,2]{0,4,5,2,3,1:T(8,128)S(1)} %slice.118, f32[256,1,4,1,8,5]{0,4,5,2,3,1:T(8,128)S(1)} %copy.92, pred[8,5]{0,1:T(8,128)(4,1)S(1)} %copy-done.5), kind=kOutput, calls=%fused_computation.18 | convolution fusion | flops 236122112 | bytes 3842088 | tf_op jit(solution)/shard_map/conv_general_dilated | solution.py:31
  108.4 0.0 collective-permute-done.8
  108.4 1.6 %collective-permute-done.9 = f32[128,1,4,32]{0,2,3,1:T(4,128)S(1)} collective-permute-done((f32[128,1,4,32]{0,2,3,1:T(4,128)S(1)}, f32[128,1,4,32]{0,2,3,1:T(4,128)S(1)}, u32[]{:S(2)}, u32[]{:S(2)}) %collective-permute-start.9) | collective-permute-done | bytes 65568 | tf_op jit(solution)/shard_map/ppermute | solution.py:27
  110.0 0.3 fusion.67
  110.3 0.7 copy.99
  (30 shorter events, 0.5 us)
Async XLA Ops:
  0.0 60.5 %copy-start = (f32[3,3,3,128,128]{4,3,2,1,0:T(8,128)S(1)}, f32[3,3,3,128,128]{4,3,2,1,0:T(8,128)}, u32[]{:S(2)}) copy-start(f32[3,3,3,128,128]{4,3,2,1,0:T(8,128)} %param.17) | copy-start | bytes 5308420
  0.0 7.6 %copy-start.2 = (f32[64,4,4,128]{3,2,1,0:T(4,128)S(1)}, f32[64,4,4,128]{3,2,1,0:T(4,128)}, u32[]{:S(2)}) copy-start(f32[64,4,4,128]{3,2,1,0:T(4,128)} %param.14) | copy-start | bytes 1572868
  1.2 6.5 %collective-permute-start = (f32[64,1,4,128]{3,0,2,1:T(8,128)S(1)}, f32[64,1,4,128]{3,0,2,1:T(8,128)S(1)}, u32[]{:S(2)}, u32[]{:S(2)}) collective-permute-start(f32[64,1,4,128]{3,0,2,1:T(8,128)S(1)} %copy.117), channel_id=1, source_target_pairs={{0,4},{4,8},{8,12},{12,16},{16,20},{20,24},{24,28},{1,5},{5,9},{9,... | collective-permute-start | bytes 393224 | tf_op jit(solution)/shard_map/ppermute | solution.py:15
  5.7 6.3 %collective-permute-start.1 = (f32[64,1,4,128]{3,0,2,1:T(8,128)S(1)}, f32[64,1,4,128]{3,0,2,1:T(8,128)S(1)}, u32[]{:S(2)}, u32[]{:S(2)}) collective-permute-start(f32[64,1,4,128]{3,0,2,1:T(8,128)S(1)} %copy.118), channel_id=1, source_target_pairs={{4,0},{8,4},{12,8},{16,12},{20,16},{24,20},{28,24},{5,1},{9,5},{13... | collective-permute-start | bytes 393224 | tf_op jit(solution)/shard_map/ppermute | solution.py:17
  12.0 5.8 %collective-permute-start.2 = (f32[64,6,1,128]{3,0,2,1:T(8,128)S(1)}, f32[64,6,1,128]{3,0,2,1:T(8,128)S(1)}, u32[]{:S(2)}, u32[]{:S(2)}) collective-permute-start(f32[64,6,1,128]{3,0,2,1:T(8,128)S(1)} %get-tuple-element.45), channel_id=1, source_target_pairs={{0,1},{1,2},{2,3},{4,5},{5,6},{6,7},{8,9},{9,10},{10,11},{12,13},{... | collective-permute-start | bytes 589832 | tf_op jit(solution)/shard_map/ppermute | solution.py:15
  15.2 6.4 %collective-permute-start.3 = (f32[64,6,1,128]{3,0,2,1:T(8,128)S(1)}, f32[64,6,1,128]{3,0,2,1:T(8,128)S(1)}, u32[]{:S(2)}, u32[]{:S(2)}) collective-permute-start(f32[64,6,1,128]{3,0,2,1:T(8,128)S(1)} %get-tuple-element.46), channel_id=1, source_target_pairs={{1,0},{2,1},{3,2},{5,4},{6,5},{7,6},{9,8},{10,9},{11,10},{13,12},{... | collective-permute-start | bytes 589832 | tf_op jit(solution)/shard_map/ppermute | solution.py:17
  29.4 1.2 %copy-start.7 = (f32[3,3,3,64,64]{4,3,2,1,0:T(8,128)S(1)}, f32[3,3,3,64,64]{4,3,2,1,0:T(8,128)}, u32[]{:S(2)}) copy-start(f32[3,3,3,64,64]{4,3,2,1,0:T(8,128)} %param.15) | copy-start | bytes 1327108
  29.4 1.2 %copy-start.8 = (pred[8,17]{0,1:T(8,128)(4,1)S(1)}, pred[8,17]{0,1:T(8,128)(4,1)}, u32[]{:S(2)}) copy-start(pred[8,17]{0,1:T(8,128)(4,1)} %constant.216) | copy-start | bytes 412
  39.8 1.0 copy-start.4
  41.4 5.9 %collective-permute-start.4 = (f32[128,1,2,64]{0,3,2,1:T(8,128)S(1)}, f32[128,1,2,64]{0,3,2,1:T(8,128)S(1)}, u32[]{:S(2)}, u32[]{:S(2)}) collective-permute-start(f32[128,1,2,64]{0,3,2,1:T(8,128)S(1)} %get-tuple-element.53), channel_id=1, source_target_pairs={{0,4},{4,8},{8,12},{12,16},{16,20},{20,24},{24,28},{1,5},{5,9},{9,... | collective-permute-start | bytes 196616 | tf_op jit(solution)/shard_map/ppermute | solution.py:15
  45.4 5.6 %collective-permute-start.5 = (f32[128,1,2,64]{0,3,2,1:T(8,128)S(1)}, f32[128,1,2,64]{0,3,2,1:T(8,128)S(1)}, u32[]{:S(2)}, u32[]{:S(2)}) collective-permute-start(f32[128,1,2,64]{0,3,2,1:T(8,128)S(1)} %get-tuple-element.54), channel_id=1, source_target_pairs={{4,0},{8,4},{12,8},{16,12},{20,16},{24,20},{28,24},{5,1},{9,5},{13... | collective-permute-start | bytes 196616 | tf_op jit(solution)/shard_map/ppermute | solution.py:17
  51.0 5.1 %collective-permute-start.6 = (f32[128,4,1,64]{0,3,2,1:T(8,128)S(1)}, f32[128,4,1,64]{0,3,2,1:T(8,128)S(1)}, u32[]{:S(2)}, u32[]{:S(2)}) collective-permute-start(f32[128,4,1,64]{0,3,2,1:T(8,128)S(1)} %get-tuple-element.49), channel_id=1, source_target_pairs={{0,1},{1,2},{2,3},{4,5},{5,6},{6,7},{8,9},{9,10},{10,11},{12,13},{... | collective-permute-start | bytes 393224 | tf_op jit(solution)/shard_map/ppermute | solution.py:15
  54.2 5.7 %collective-permute-start.7 = (f32[128,4,1,64]{0,3,2,1:T(8,128)S(1)}, f32[128,4,1,64]{0,3,2,1:T(8,128)S(1)}, u32[]{:S(2)}, u32[]{:S(2)}) collective-permute-start(f32[128,4,1,64]{0,3,2,1:T(8,128)S(1)} %get-tuple-element.50), channel_id=1, source_target_pairs={{1,0},{2,1},{3,2},{5,4},{6,5},{7,6},{9,8},{10,9},{11,10},{13,12},{... | collective-permute-start | bytes 393224 | tf_op jit(solution)/shard_map/ppermute | solution.py:17
  60.3 0.7 copy-start.6
  63.2 14.6 %copy-start.3 = (f32[2,2,2,128,64]{3,4,2,1,0:T(8,128)S(1)}, f32[2,2,2,128,64]{3,4,2,1,0:T(8,128)}, u32[]{:S(2)}) copy-start(f32[2,2,2,128,64]{3,4,2,1,0:T(8,128)} %param.18) | copy-start | bytes 786436
  78.2 13.2 %copy-start.5 = (pred[8,5]{0,1:T(8,128)(4,1)S(1)}, pred[8,5]{0,1:T(8,128)(4,1)}, u32[]{:S(2)}) copy-start(pred[8,5]{0,1:T(8,128)(4,1)} %constant.213) | copy-start | bytes 124
  91.3 15.0 %copy-start.1 = (f32[3,3,3,256,128]{4,3,2,1,0:T(8,128)S(1)}, f32[3,3,3,256,128]{4,3,2,1,0:T(8,128)}, u32[]{:S(2)}) copy-start(f32[3,3,3,256,128]{4,3,2,1,0:T(8,128)} %param.19) | copy-start | bytes 10616836
  95.6 12.8 %collective-permute-start.8 = (f32[128,1,4,32]{0,2,3,1:T(4,128)S(1)}, f32[128,1,4,32]{0,2,3,1:T(4,128)S(1)}, u32[]{:S(2)}, u32[]{:S(2)}) collective-permute-start(f32[128,1,4,32]{0,2,3,1:T(4,128)S(1)} %slice_bitcast_fusion.1), channel_id=1, source_target_pairs={{0,4},{4,8},{8,12},{12,16},{16,20},{20,24},{24,28},{1,5},{5,9},{9,... | collective-permute-start | bytes 196616 | tf_op jit(solution)/shard_map/ppermute | solution.py:27
  104.4 5.6 %collective-permute-start.9 = (f32[128,1,4,32]{0,2,3,1:T(4,128)S(1)}, f32[128,1,4,32]{0,2,3,1:T(4,128)S(1)}, u32[]{:S(2)}, u32[]{:S(2)}) collective-permute-start(f32[128,1,4,32]{0,2,3,1:T(4,128)S(1)} %slice_bitcast_fusion), channel_id=1, source_target_pairs={{4,0},{8,4},{12,8},{16,12},{20,16},{24,20},{28,24},{5,1},{9,5},{13... | collective-permute-start | bytes 196616 | tf_op jit(solution)/shard_map/ppermute | solution.py:27

commit v2 on v1

v2 whole, which is shorter than its diff:
```python
import functools

import jax
import jax.numpy as jnp
from jax import lax
from jax.experimental import pallas as pl
from jax.experimental.pallas import tpu as pltpu
from jax.sharding import PartitionSpec as P

MESH = pl.DeviceIdType.MESH
F32, BF16 = jnp.float32, jnp.bfloat16
WAYS = ((1, 0), (-1, 0), (0, 1), (0, -1), (1, 1), (1, -1), (-1, 1), (-1, -1))


def split(x):
    high = x.astype(BF16)
    return high, (x - high.astype(F32)).astype(BF16)


def dot3(a, b, dims=(((1,), (0,)), ((), ()))):
    dot = functools.partial(lax.dot_general, dimension_numbers=dims, preferred_element_type=F32)
    return dot(a[0], b[0]) + dot(a[1], b[0]) + dot(a[0], b[1])


def gelu(x):
    return 0.5 * x * (1.0 + lax.erf(x * (0.5**0.5)))


def beside(x, span):
    at = lax.rem(lax.broadcasted_iota(jnp.int32, x.shape, 0), span)
    before = jnp.where(at == 0, 0.0, pltpu.roll(x, 1, 0))
    after = jnp.where(at == span - 1, 0.0, pltpu.roll(x, x.shape[0] - 1, 0))
    return before, after


def kernel(
    slabs, groups,
    vol, fine, down1_hbm, middle_hbm, shard, coarse_hbm,
    out,
    field, pair, rows_h, rows_l, fine_h, fine_l, down1, middle, middle_h, middle_l,
    second, rows2_h, rows2_l, level2, gathered, coarse_w, coarse_h, coarse_l,
    coarse, taps_h, taps_l, upward, downward, from_lower, from_upper,
    load_sem, send1, recv1, send2, recv2, wsend, wrecv, fsend, frecv, csend, crecv, psend, precv,
):
    s, g = lax.axis_index("slab"), lax.axis_index("grp")
    depth, height, chans, width = vol.shape
    half = width // 2

    loads = [
        pltpu.make_async_copy(down1_hbm, down1, load_sem.at[0]),
        pltpu.make_async_copy(middle_hbm, middle, load_sem.at[1]),
        pltpu.make_async_copy(coarse_hbm, coarse_w, load_sem.at[2]),
    ]
    for load in loads:
        load.start()

    def exists(ds, dg):
        return (s + ds >= 0) & (s + ds < slabs) & (g + dg >= 0) & (g + dg < groups)

    barrier = pltpu.get_barrier_semaphore()
    heard = jnp.int32(0)
    for ds, dg in WAYS:
        there = exists(ds, dg)
        heard = heard + there.astype(jnp.int32)

        @pl.when(there)
        def _():
            pl.semaphore_signal(barrier, inc=1, device_id=(s + ds, g + dg), device_id_type=MESH)

    for dg in range(2, groups):
        for sign in (1, -1):
            there = exists(0, sign * dg)
            heard = heard + there.astype(jnp.int32)

            @pl.when(there)
            def _():
                pl.semaphore_signal(barrier, inc=1, device_id=(s, g + sign * dg), device_id_type=MESH)

    pl.semaphore_wait(barrier, heard)

    def part(way, size, offset):
        if way == 0:
            return pl.ds(offset, size)
        return pl.ds(offset + (size - 1 if way > 0 else 0), 1)

    def landing(way, size):
        if way == 0:
            return pl.ds(1, size)
        return pl.ds(0 if way > 0 else size + 1, 1)

    def halo(src, offset, buf, sends, recvs):
        nd, nh = buf.shape[0] - 2, buf.shape[1] - 2
        copies = []
        for k, (ds, dg) in enumerate(WAYS):
            copies.append(
                pltpu.make_async_remote_copy(
                    src_ref=src.at[part(ds, nd, offset), part(dg, nh, offset)],
                    dst_ref=buf.at[landing(ds, nd), landing(dg, nh)],
                    send_sem=sends.at[k],
                    recv_sem=recvs.at[k],
                    device_id=(s + ds, g + dg),
                    device_id_type=MESH,
                )
            )

            @pl.when(exists(ds, dg))
            def _():
                copies[k].start()

            @pl.when(jnp.logical_not(exists(-ds, -dg)))
            def _():
                piece = (landing(ds, nd), landing(dg, nh))
                shape = (piece[0].size, piece[1].size) + buf.shape[2:]
                buf[piece[0], piece[1]] = jnp.zeros(shape, F32)

        return copies

    def arrive(copies, received):
        for k, (ds, dg) in enumerate(WAYS):
            if received:
                @pl.when(exists(-ds, -dg))
                def _():
                    copies[k].wait_recv()
            else:
                @pl.when(exists(ds, dg))
                def _():
                    copies[k].wait_send()

    first = halo(vol, 0, field, send1, recv1)

    part_rows = shard.shape[0] // 2
    mine = pl.ds(pl.multiple_of(lax.rem(s, 2) * part_rows, part_rows), part_rows)
    sibling = s + 1 - 2 * lax.rem(s, 2)
    spread = []
    for j in range(1, groups):
        copy = pltpu.make_async_remote_copy(
            src_ref=shard.at[mine],
            dst_ref=gathered.at[g, mine],
            send_sem=wsend.at[j],
            recv_sem=wrecv.at[j],
            device_id=(s, lax.rem(g + j, groups)),
            device_id_type=MESH,
        )
        copy.start()
        spread.append(copy)
    gathered[pl.ds(g, 1)] = shard[...][None]

    blank = jnp.zeros((chans, 2 * chans), BF16)
    nothing = jnp.zeros((chans, chans), F32)
    for a in range(3):
        for b in range(3):
            for pos in range(4):
                left = fine[(a * 3 + b) * 3 + pos] if pos < 3 else nothing
                right = fine[(a * 3 + b) * 3 + pos - 1] if pos > 0 else nothing
                high, low = split(jnp.concatenate([left, right], axis=1))
                for hb in range(2):
                    p, sub = divmod(b + hb, 2)
                    spot = pl.ds((pos * 2 + sub) * chans, chans)
                    fine_h[a, p, spot, hb * 2 * chans : (hb + 1) * 2 * chans] = high
                    fine_l[a, p, spot, hb * 2 * chans : (hb + 1) * 2 * chans] = low
        for pos in range(4):
            for p, sub, hb in ((0, 0, 1), (1, 1, 0)):
                spot = pl.ds((pos * 2 + sub) * chans, chans)
                fine_h[a, p, spot, hb * 2 * chans : (hb + 1) * 2 * chans] = blank
                fine_l[a, p, spot, hb * 2 * chans : (hb + 1) * 2 * chans] = blank

    loads[1].wait()

    @pl.loop(0, 9)
    def _(t):
        middle_h[t], middle_l[t] = split(middle[t])

    field[1 : depth + 1, 1 : height + 1] = vol[...]
    arrive(first, True)

    pairs = height // 2 + 1

    @pl.loop(0, depth + 2)
    def _(d):
        for p in range(pairs):
            both = field[d, 2 * p : 2 * p + 2].reshape(2 * chans, width)
            pair[p] = both.T
        for p in range(pairs):
            even = pair[p, pl.ds(0, half, stride=2), :]
            odd = pair[p, pl.ds(1, half, stride=2), :]
            before, _ = beside(odd, half)
            _, after = beside(even, half)
            rows_h[d, p], rows_l[d, p] = split(jnp.concatenate([before, even, odd, after], axis=1))

    blocks = height // 2
    total = None
    for a in range(3):
        for p in range(2):
            lhs = [
                r[a : a + depth, p : p + blocks].reshape(depth * blocks * half, 8 * chans) for r in (rows_h, rows_l)
            ]
            term = dot3(lhs, (fine_h[a, p], fine_l[a, p]))
            total = term if total is None else total + term
    one = gelu(total).reshape(depth // 2, 2, blocks * half, 4 * chans)
    loads[0].wait()
    total = None
    for a in range(2):
        lhs = one[:, a].reshape(depth // 2 * blocks * half, 4 * chans)
        term = dot3(split(lhs), split(down1[a]))
        total = term if total is None else total + term
    d2, h2, c2 = depth // 2, blocks, total.shape[1]
    second[1 : d2 + 1, 1 : h2 + 1] = total.reshape(d2, h2, half, c2)
    again = halo(second, 1, second, send2, recv2)

    forward = []
    for j in range(1, groups):
        spread[j - 1].wait_recv()
        source = lax.rem(g + groups - j, groups)
        copy = pltpu.make_async_remote_copy(
            src_ref=gathered.at[source, mine],
            dst_ref=gathered.at[source, mine],
            send_sem=fsend.at[j],
            recv_sem=frecv.at[j],
            device_id=(sibling, g),
            device_id_type=MESH,
        )
        copy.start()
        forward.append(copy)

    loads[2].wait()

    @pl.loop(0, 9)
    def _(t):
        coarse_h[t], coarse_l[t] = split(coarse_w[t])

    arrive(again, True)

    @pl.loop(0, d2 + 2)
    def _(d):
        for h in range(h2 + 2):
            x = second[d, h]
            before, after = beside(x, half)
            rows2_h[d, h], rows2_l[d, h] = split(jnp.concatenate([before, x, after], axis=1))

    total = None
    for a in range(3):
        for b in range(3):
            lhs = [r[a : a + d2, b : b + h2].reshape(d2 * h2 * half, 3 * c2) for r in (rows2_h, rows2_l)]
            term = dot3(lhs, (middle_h[a * 3 + b], middle_l[a * 3 + b]))
            total = term if total is None else total + term
    level2[...] = gelu(total)
    quarter = half // 2
    lhs = jnp.concatenate(
        [level2[pl.ds(r * half + c, quarter, stride=2), :] for r in range(d2 * h2) for c in range(2)], axis=1
    )
    for copy in forward:
        copy.wait_recv()
    weights = gathered[...].reshape(groups * shard.shape[0], shard.shape[1])
    share = dot3(split(lhs), split(weights), (((1,), (1,)), ((), ())))
    coarse[pl.ds(g, 1)] = share[None]
    sent = []
    for j in range(1, groups):
        copy = pltpu.make_async_remote_copy(
            src_ref=coarse.at[g],
            dst_ref=coarse.at[g],
            send_sem=csend.at[j],
            recv_sem=crecv.at[j],
            device_id=(s, lax.rem(g + j, groups)),
            device_id_type=MESH,
        )
        copy.start()
        sent.append(copy)
    cells = groups * quarter
    edge = jnp.zeros((quarter, taps_h.shape[1]), BF16)
    for taps in (taps_h, taps_l):
        taps[0:quarter] = edge
        taps[quarter + cells : 2 * quarter + cells] = edge
    for copy in sent:
        copy.wait_recv()
    x = coarse[...].reshape(cells, coarse.shape[2])
    before, after = beside(x, quarter)
    high, low = split(jnp.concatenate([before, x, after], axis=1))
    taps_h[quarter : quarter + cells] = high
    taps_l[quarter : quarter + cells] = low

    def plane(a):
        total = None
        for b in range(3):
            lhs = [t[b * quarter : b * quarter + cells] for t in (taps_h, taps_l)]
            term = dot3(lhs, (coarse_h[a * 3 + b], coarse_l[a * 3 + b]))
            total = term if total is None else total + term
        return total

    upward[...] = plane(0)
    up = pltpu.make_async_remote_copy(
        src_ref=upward, dst_ref=from_lower, send_sem=psend.at[0], recv_sem=precv.at[0],
        device_id=(s + 1, g), device_id_type=MESH,
    )
    down = pltpu.make_async_remote_copy(
        src_ref=downward, dst_ref=from_upper, send_sem=psend.at[1], recv_sem=precv.at[1],
        device_id=(s - 1, g), device_id_type=MESH,
    )

    @pl.when(exists(1, 0))
    def _():
        up.start()

    @pl.when(jnp.logical_not(exists(-1, 0)))
    def _():
        from_lower[...] = jnp.zeros(from_lower.shape, F32)

    downward[...] = plane(2)

    @pl.when(exists(-1, 0))
    def _():
        down.start()

    @pl.when(jnp.logical_not(exists(1, 0)))
    def _():
        from_upper[...] = jnp.zeros(from_upper.shape, F32)

    centre = plane(1)

    @pl.when(exists(-1, 0))
    def _():
        up.wait_recv()

    @pl.when(exists(1, 0))
    def _():
        down.wait_recv()

    out[...] = gelu(centre + from_lower[...] + from_upper[...]).T

    arrive(first, False)
    arrive(again, False)
    for copy in spread + forward + sent:
        copy.wait_send()

    @pl.when(exists(1, 0))
    def _():
        up.wait_send()

    @pl.when(exists(-1, 0))
    def _():
        down.wait_send()


def per_device(slabs, groups, volume, conv_fine, down_first, conv_middle, down_second, conv_coarse):
    c1, depth, height, width = volume.shape
    c2, c3, c4 = down_first.shape[4], conv_coarse.shape[3], conv_coarse.shape[4]
    half, quarter = width // 2, width // 4
    d2, h2 = depth // 2, height // 2
    part = down_second.shape[4]
    cells = groups * quarter
    vol = jnp.transpose(volume, (1, 2, 0, 3))
    fine = conv_fine.reshape(27, c1, c1)
    down1 = down_first.reshape(2, 4 * c1, c2)
    middle = conv_middle.reshape(9, 3 * c2, c2)
    shard = down_second.reshape(8 * c2, part).T
    coarse_w = conv_coarse.reshape(9, 3 * c3, c4)
    V = pltpu.VMEM
    vmem, away = pl.BlockSpec(memory_space=pltpu.VMEM), pl.BlockSpec(memory_space=pl.ANY)
    dma = pltpu.SemaphoreType.DMA
    result = pl.pallas_call(
        functools.partial(kernel, slabs, groups),
        out_shape=jax.ShapeDtypeStruct((c4, cells), F32),
        in_specs=[vmem, vmem, away, away, vmem, away],
        out_specs=vmem,
        scratch_shapes=[
            V((depth + 2, height + 2, c1, width), F32),
            V((h2 + 1, width, 2 * c1), F32),
            V((depth + 2, h2 + 1, half, 8 * c1), BF16),
            V((depth + 2, h2 + 1, half, 8 * c1), BF16),
            V((3, 2, 8 * c1, 4 * c1), BF16),
            V((3, 2, 8 * c1, 4 * c1), BF16),
            V(down1.shape, F32),
            V(middle.shape, F32),
            V(middle.shape, BF16),
            V(middle.shape, BF16),
            V((d2 + 2, h2 + 2, half, c2), F32),
            V((d2 + 2, h2 + 2, half, 3 * c2), BF16),
            V((d2 + 2, h2 + 2, half, 3 * c2), BF16),
            V((d2 * h2 * half, c2), F32),
            V((groups,) + shard.shape, F32),
            V(coarse_w.shape, F32),
            V(coarse_w.shape, BF16),
            V(coarse_w.shape, BF16),
            V((groups, quarter, c3), F32),
            V((cells + 2 * quarter, 3 * c3), BF16),
            V((cells + 2 * quarter, 3 * c3), BF16),
            V((cells, c4), F32),
            V((cells, c4), F32),
            V((cells, c4), F32),
            V((cells, c4), F32),
            dma((3,)),
            dma((8,)), dma((8,)), dma((8,)), dma((8,)),
            dma((groups,)), dma((groups,)), dma((groups,)), dma((groups,)), dma((groups,)), dma((groups,)),
            dma((2,)), dma((2,)),
        ],
        compiler_params=pltpu.CompilerParams(
            collective_id=0, has_side_effects=True, vmem_limit_bytes=60 * 1024 * 1024
        ),
    )(vol, fine, down1, middle, shard, coarse_w)
    return result.reshape(c4, 1, cells)


def solution(mesh):
    placed = (
        P(None, "slab", "grp", None),
        P(),
        P(),
        P(),
        P(None, None, None, None, "grp"),
        P(None, None, None, None, "grp"),
    )
    body = functools.partial(per_device, mesh.shape["slab"], mesh.shape["grp"])
    return jax.shard_map(
        body, mesh=mesh, in_specs=placed, out_specs=P("grp", "slab", None), check_vma=False
    )
```

time: 112 us -> 48.1 us (0.43)
  Pallas kernels: 0 us -> 42.3 us
  starting transfers between devices: 32 us -> 0 us
  blocking collectives: 27.2 us -> 0 us
  waiting for transfers between devices: 19 us -> 0 us
  matrix products: 17.7 us -> 0 us
  local copies, waits for them, and re-layouts: 14 us -> 5.54 us
    pallas_call x0 -> x1, Pallas kernels: none -> 42.3 us  [per_device(): pl.pallas_call(functools.partial(kernel, slabs, groups), out_shape=jax.Sh...]
    ppermute x10 -> x0, starting transfers between devices: 32 us -> none  [the longest x4 14.8 us: padded_2(): lax.ppermute(tail, axis, [(i, (i + 1) % count) for i in range(ends)])]
    all_gather x2 -> x0, blocking collectives: 27.2 us -> none  [the longest x1 14.4 us: per_device(): gathered = lax.all_gather(level_two, 'grp', axis=2, tiled=True)]
    ppermute x10 -> x0, waiting for transfers between devices: 19 us -> none  [the longest x4 15.4 us: padded_2(): lax.ppermute(head, axis, [((i + 1) % count, i) for i in range(ends)])]
    conv_general_dilated x7 -> x0, matrix products: 17.7 us -> none  [convolve(): lax.conv_general_dilated(field[None], kernel, (stride, stride, stride), p...]
    broadcast_in_dim x3 -> x0, local copies, waits for them, and re-layouts: 3.48 us -> none  [convolve(): field[None]]
    unnamed x25 -> x3, local copies, waits for them, and re-layouts: 6.57 us -> 4.63 us
    mul x10 -> x0, local copies, waits for them, and re-layouts: 1.35 us -> none  [the longest x4 1.16 us: per_device(): jax.nn.gelu(convolve(padded, conv_fine, 1, sideways), approximate=False)]
  transfers between devices with their start and end apart: 10 -> 0, of which waited for: 7 -> 0; matrix products, arithmetic and copies ran while one was open for 2% -> 0% of each run, Pallas kernels for 0% -> 0%
where the time goes in v2:
time: 48.1 us; the launch traced here: 47.8 us
  Pallas kernels  42.3 us (88%)
  local copies, waits for them, and re-layouts  5.54 us (12%)
    pallas_call x1, Pallas kernels, per_device(): pl.pallas_call(functools.partial(kernel, slabs, groups), out_shape=jax.Sh...  42.3 us
    unnamed x3, local copies, waits for them, and re-layouts  4.63 us

profile of v2, /device:TPU:1, one launch (start us, length us, event | category | flops | bytes accessed | tf_op | source)
XLA Modules:
  0.0 47.8 jit_solution(11534156852478081261)
XLA Ops:
  0.0 1.2 %copy.8 = f32[2,2,2,128,64]{3,2,1,0,4:T(2,128)S(1)} copy(f32[2,2,2,128,64]{3,4,2,1,0:T(8,128)} %param.10) | data formatting | bytes 524288 | tf_op args[4]
  1.2 0.9 %reshape.21 = f32[1024,64]{0,1:T(8,128)} reshape(f32[2,2,2,128,64]{3,2,1,0,4:T(2,128)S(1)} %copy.8) | data formatting | bytes 524288 | tf_op jit(solution)/shard_map/reshape | solution.py:354
  2.1 2.0 %copy.11 = f32[64,4,4,128]{3,0,2,1:T(8,128)} copy(f32[64,4,4,128]{3,2,1,0:T(4,128)} %param.6) | data formatting | bytes 1048576 | tf_op args[0]
  4.1 42.3 %shard_map.64 = f32[128,128]{1,0:T(8,128)} custom-call(f32[4,4,64,128]{3,2,1,0:T(8,128)} %bitcast.14, f32[27,64,64]{2,1,0:T(8,128)} %bitcast.17, f32[2,256,128]{2,1,0:T(8,128)} %bitcast.19, f32[9,384,128]{2,1,0:T(8,128)} %bitcast.15, f32[64,1024]{1,0:T(8,128)} %bitcast.16, f32[9,768,128]{2,1,0:T(8,128)} %bitcast.13), custom_call_target="tpu_custom_call" | custom-call | tf_op jit(solution)/shard_map/pallas_call | solution.py:359
  46.4 1.5 %copy.13 = f32[128,1,128]{2,1,0:T(1,128)} copy(f32[128,1,128]{2,1,0:T(1,128)} %bitcast.18) | data formatting | bytes 131072

commit v3 on v2

v3 whole, which is shorter than its diff:
```python
import functools

import jax
import jax.numpy as jnp
from jax import lax
from jax.experimental import pallas as pl
from jax.experimental.pallas import tpu as pltpu
from jax.sharding import PartitionSpec as P

MESH = pl.DeviceIdType.MESH
F32, BF16 = jnp.float32, jnp.bfloat16
WAYS = ((1, 0), (-1, 0), (0, 1), (0, -1), (1, 1), (1, -1), (-1, 1), (-1, -1))


def split(x):
    high = x.astype(BF16)
    return high, (x - high.astype(F32)).astype(BF16)


def stacked(x):
    return jnp.concatenate(split(x), axis=0)


def product(both, weights, dims=(((1,), (0,)), ((), ()))):
    dot = functools.partial(lax.dot_general, dimension_numbers=dims, preferred_element_type=F32)
    rows = both.shape[0] // 2
    wide = dot(both, weights[0])
    return wide[:rows] + wide[rows:] + dot(both[:rows], weights[1])


def plus(total, term):
    return term if total is None else total + term


def gelu(x):
    return 0.5 * x * (1.0 + lax.erf(x * (0.5**0.5)))


def beside(x, span):
    at = lax.rem(lax.broadcasted_iota(jnp.int32, x.shape, 0), span)
    before = jnp.where(at == 0, 0.0, pltpu.roll(x, 1, 0))
    after = jnp.where(at == span - 1, 0.0, pltpu.roll(x, x.shape[0] - 1, 0))
    return before, after


def kernel(
    slabs, groups,
    vol, fine, down1_hbm, middle_hbm, shard, coarse_hbm,
    out,
    field, pair, rows, fine_h, fine_l, down1, down1_h, down1_l, middle, middle_h, middle_l,
    second, rows2, level2, gathered, coarse_w, edges_h, edges_l, centre_h, centre_l,
    coarse, taps, upward, downward, from_lower, from_upper,
    load_sem, send1, recv1, send2, recv2, wsend, wrecv, xsend, xrecv, fsend, frecv, csend, crecv, psend, precv,
):
    s, g = lax.axis_index("slab"), lax.axis_index("grp")
    depth, height, chans, width = (field.shape[0] - 2, field.shape[1] - 2) + field.shape[2:]
    half = width // 2

    loads = [
        pltpu.make_async_copy(down1_hbm, down1, load_sem.at[0]),
        pltpu.make_async_copy(middle_hbm, middle, load_sem.at[1]),
        pltpu.make_async_copy(coarse_hbm, coarse_w, load_sem.at[2]),
    ]
    for load in loads:
        load.start()

    def exists(ds, dg):
        return (s + ds >= 0) & (s + ds < slabs) & (g + dg >= 0) & (g + dg < groups)

    lines = depth * height
    for r in range(lines):
        field[1 + r // height, 1 + r % height] = vol[pl.ds(r, chans, stride=lines), :]

    barrier = pltpu.get_barrier_semaphore()
    heard = jnp.int32(0)
    for ds, dg in WAYS:
        there = exists(ds, dg)
        heard = heard + there.astype(jnp.int32)

        @pl.when(there)
        def _():
            pl.semaphore_signal(barrier, inc=1, device_id=(s + ds, g + dg), device_id_type=MESH)

    for dg in range(2, groups):
        for sign in (1, -1):
            there = exists(0, sign * dg)
            heard = heard + there.astype(jnp.int32)

            @pl.when(there)
            def _():
                pl.semaphore_signal(barrier, inc=1, device_id=(s, g + sign * dg), device_id_type=MESH)

    sibling = s + 1 - 2 * lax.rem(s, 2)
    across = s + 2 - 4 * lax.rem(s // 2, 2)
    pl.semaphore_signal(barrier, inc=1, device_id=(across, g), device_id_type=MESH)
    pl.semaphore_wait(barrier, heard + 1)

    def part(way, size, offset):
        if way == 0:
            return pl.ds(offset, size)
        return pl.ds(offset + (size - 1 if way > 0 else 0), 1)

    def landing(way, size):
        if way == 0:
            return pl.ds(1, size)
        return pl.ds(0 if way > 0 else size + 1, 1)

    def halo(src, offset, buf, sends, recvs):
        nd, nh = buf.shape[0] - 2, buf.shape[1] - 2
        copies = []
        for k, (ds, dg) in enumerate(WAYS):
            copies.append(
                pltpu.make_async_remote_copy(
                    src_ref=src.at[part(ds, nd, offset), part(dg, nh, offset)],
                    dst_ref=buf.at[landing(ds, nd), landing(dg, nh)],
                    send_sem=sends.at[k],
                    recv_sem=recvs.at[k],
                    device_id=(s + ds, g + dg),
                    device_id_type=MESH,
                )
            )

            @pl.when(exists(ds, dg))
            def _():
                copies[k].start()

            @pl.when(jnp.logical_not(exists(-ds, -dg)))
            def _():
                piece = (landing(ds, nd), landing(dg, nh))
                shape = (piece[0].size, piece[1].size) + buf.shape[2:]
                buf[piece[0], piece[1]] = jnp.zeros(shape, F32)

        return copies

    def arrive(copies, received, ways=range(len(WAYS))):
        for k in ways:
            ds, dg = WAYS[k]
            if received:
                @pl.when(exists(-ds, -dg))
                def _():
                    copies[k].wait_recv()
            else:
                @pl.when(exists(ds, dg))
                def _():
                    copies[k].wait_send()

    first = halo(field, 1, field, send1, recv1)

    taps_of = shard.shape[0]
    parity, bit = lax.rem(s, 2), lax.rem(s // 2, 2)
    quarter_taps = pl.ds((parity * 2 + bit) * (taps_of // 4), taps_of // 4)
    half_taps = pl.ds(parity * (taps_of // 2), taps_of // 2)
    spread, crossed, forward = [], [], []
    for j in range(1, groups):
        copy = pltpu.make_async_remote_copy(
            src_ref=shard.at[quarter_taps],
            dst_ref=gathered.at[g, quarter_taps],
            send_sem=wsend.at[j],
            recv_sem=wrecv.at[j],
            device_id=(s, lax.rem(g + j, groups)),
            device_id_type=MESH,
        )
        copy.start()
        spread.append(copy)

    def hand_on(arrived, out_copies, piece, sends, recvs, peer):
        for j in range(1, groups):
            arrived[j - 1].wait_recv()
            source = lax.rem(g + groups - j, groups)
            copy = pltpu.make_async_remote_copy(
                src_ref=gathered.at[source, piece],
                dst_ref=gathered.at[source, piece],
                send_sem=sends.at[j],
                recv_sem=recvs.at[j],
                device_id=(peer, g),
                device_id_type=MESH,
            )
            copy.start()
            out_copies.append(copy)

    gathered[pl.ds(g, 1)] = shard[...][None]

    blank = jnp.zeros((chans, 2 * chans), BF16)
    nothing = jnp.zeros((chans, chans), F32)
    for a in range(3):
        for b in range(3):
            for pos in range(4):
                left = fine[(a * 3 + b) * 3 + pos] if pos < 3 else nothing
                right = fine[(a * 3 + b) * 3 + pos - 1] if pos > 0 else nothing
                high, low = split(jnp.concatenate([left, right], axis=1))
                for hb in range(2):
                    p, sub = divmod(b + hb, 2)
                    spot = pl.ds((pos * 2 + sub) * chans, chans)
                    fine_h[a, p, spot, hb * 2 * chans : (hb + 1) * 2 * chans] = high
                    fine_l[a, p, spot, hb * 2 * chans : (hb + 1) * 2 * chans] = low
        for pos in range(4):
            for p, sub, hb in ((0, 0, 1), (1, 1, 0)):
                spot = pl.ds((pos * 2 + sub) * chans, chans)
                fine_h[a, p, spot, hb * 2 * chans : (hb + 1) * 2 * chans] = blank
                fine_l[a, p, spot, hb * 2 * chans : (hb + 1) * 2 * chans] = blank

    pairs = height // 2 + 1
    blocks = height // 2
    d2, h2, c2 = depth // 2, blocks, down1.shape[2]
    for load in loads:
        load.wait()
    for a in range(2):
        down1_h[a], down1_l[a] = split(down1[a])

    @pl.loop(0, 3)
    def _(a):
        for b in range(3):
            high, low = split(middle[a * 3 + b])
            for hb in range(2):
                spot = pl.ds((b + hb) * 3 * c2, 3 * c2)
                middle_h[a, spot, hb * c2 : (hb + 1) * c2] = high
                middle_l[a, spot, hb * c2 : (hb + 1) * c2] = low

    outs = coarse_w.shape[2]

    @pl.loop(0, 3)
    def _(b):
        for a, k in ((0, 0), (2, 1)):
            high, low = split(coarse_w[a * 3 + b])
            edges_h[b, :, k * outs : (k + 1) * outs] = high
            edges_l[b, :, k * outs : (k + 1) * outs] = low
        centre_h[b], centre_l[b] = split(coarse_w[3 + b])

    def build(p):
        @pl.loop(0, depth + 2)
        def _(d):
            pair[p] = field[d, 2 * p : 2 * p + 2].reshape(2 * chans, width).T
            even = pair[p, pl.ds(0, half, stride=2), :]
            odd = pair[p, pl.ds(1, half, stride=2), :]
            before, _ = beside(odd, half)
            _, after = beside(even, half)
            rows[0, d, p], rows[1, d, p] = split(jnp.concatenate([before, even, odd, after], axis=1))

    totals = [None] * blocks

    def convolve(p):
        for a in range(3):
            lhs = rows[:, a : a + depth, p].reshape(2 * depth * half, 8 * chans)
            for block in range(blocks):
                if 0 <= p - block <= 1:
                    w = (fine_h[a, p - block], fine_l[a, p - block])
                    totals[block] = plus(totals[block], product(lhs, w))

    arrive(first, True, range(0, 2))
    for p in range(1, blocks):
        build(p)
        convolve(p)
    arrive(first, True, range(2, len(WAYS)))
    for p in (0, blocks):
        build(p)
        convolve(p)
    ones = [gelu(t).reshape(d2, 2, half, 4 * chans) for t in totals]
    total = None
    for a in range(2):
        lhs = jnp.concatenate([o[:, a].reshape(d2 * half, 4 * chans) for o in ones], axis=0)
        total = plus(total, product(stacked(lhs), (down1_h[a], down1_l[a])))
    total = total.reshape(h2, d2, half, c2)
    for h in range(h2):
        second[1 : d2 + 1, 1 + h] = total[h]
    again = halo(second, 1, second, send2, recv2)
    hand_on(spread, crossed, quarter_taps, xsend, xrecv, across)

    def widen(h):
        @pl.loop(0, d2 + 2)
        def _(d):
            x = second[d, h]
            before, after = beside(x, half)
            spot = slice(h * 3 * c2, (h + 1) * 3 * c2)
            rows2[0, d, :, spot], rows2[1, d, :, spot] = split(jnp.concatenate([before, x, after], axis=1))

    def middle_term(a, low, high, left, right):
        lhs = rows2[:, a : a + d2, :, low:high].reshape(2 * d2 * half, high - low)
        return product(lhs, (middle_h[a, low:high, left:right], middle_l[a, low:high, left:right]))

    k3 = 3 * c2
    arrive(again, True, range(0, 2))
    for h in range(1, h2 + 1):
        widen(h)
    total, sides = None, [None, None]
    for a in range(3):
        total = plus(total, middle_term(a, k3, 3 * k3, 0, 2 * c2))
    arrive(again, True, range(2, len(WAYS)))
    for h in (0, h2 + 1):
        widen(h)
    for a in range(3):
        sides[0] = plus(sides[0], middle_term(a, 0, k3, 0, c2))
        sides[1] = plus(sides[1], middle_term(a, 3 * k3, 4 * k3, c2, 2 * c2))
    hand_on(crossed, forward, half_taps, fsend, frecv, sibling)
    for h in range(h2):
        level2[h] = gelu(total[:, h * c2 : (h + 1) * c2] + sides[h])
    quarter = half // 2
    lhs = jnp.concatenate(
        [
            level2[h, pl.ds(d * half + c, quarter, stride=2), :]
            for d in range(d2) for h in range(h2) for c in range(2)
        ],
        axis=1,
    )
    lhs = stacked(lhs)
    for copy in forward:
        copy.wait_recv()
    weights = jnp.concatenate(
        [gathered[:, t].reshape(groups * shard.shape[1], c2) for t in range(taps_of)], axis=1
    )
    share = product(lhs, split(weights), (((1,), (1,)), ((), ())))
    coarse[pl.ds(g, 1)] = share[None]
    sent = []
    for j in range(1, groups):
        copy = pltpu.make_async_remote_copy(
            src_ref=coarse.at[g],
            dst_ref=coarse.at[g],
            send_sem=csend.at[j],
            recv_sem=crecv.at[j],
            device_id=(s, lax.rem(g + j, groups)),
            device_id_type=MESH,
        )
        copy.start()
        sent.append(copy)
    cells = groups * quarter
    edge = jnp.zeros((2, quarter, taps.shape[2]), BF16)
    taps[:, 0:quarter] = edge
    taps[:, quarter + cells : 2 * quarter + cells] = edge
    for copy in sent:
        copy.wait_recv()
    x = coarse[...].reshape(cells, coarse.shape[2])
    before, after = beside(x, quarter)
    taps[0, quarter : quarter + cells], taps[1, quarter : quarter + cells] = split(
        jnp.concatenate([before, x, after], axis=1)
    )

    def plane(high, low):
        total = None
        for b in range(3):
            lhs = taps[:, b * quarter : b * quarter + cells].reshape(2 * cells, taps.shape[2])
            total = plus(total, product(lhs, (high[b], low[b])))
        return total

    both = plane(edges_h, edges_l)
    upward[...] = both[:, :outs]
    downward[...] = both[:, outs:]
    up = pltpu.make_async_remote_copy(
        src_ref=upward, dst_ref=from_lower, send_sem=psend.at[0], recv_sem=precv.at[0],
        device_id=(s + 1, g), device_id_type=MESH,
    )
    down = pltpu.make_async_remote_copy(
        src_ref=downward, dst_ref=from_upper, send_sem=psend.at[1], recv_sem=precv.at[1],
        device_id=(s - 1, g), device_id_type=MESH,
    )

    @pl.when(exists(1, 0))
    def _():
        up.start()

    @pl.when(jnp.logical_not(exists(-1, 0)))
    def _():
        from_lower[...] = jnp.zeros(from_lower.shape, F32)

    @pl.when(exists(-1, 0))
    def _():
        down.start()

    @pl.when(jnp.logical_not(exists(1, 0)))
    def _():
        from_upper[...] = jnp.zeros(from_upper.shape, F32)

    centre = plane(centre_h, centre_l)

    @pl.when(exists(-1, 0))
    def _():
        up.wait_recv()

    @pl.when(exists(1, 0))
    def _():
        down.wait_recv()

    out[...] = gelu(centre + from_lower[...] + from_upper[...]).T

    arrive(first, False)
    arrive(again, False)
    for copy in spread + crossed + forward + sent:
        copy.wait_send()

    @pl.when(exists(1, 0))
    def _():
        up.wait_send()

    @pl.when(exists(-1, 0))
    def _():
        down.wait_send()


def per_device(slabs, groups, volume, conv_fine, down_first, conv_middle, down_second, conv_coarse):
    c1, depth, height, width = volume.shape
    c2, c3, c4 = down_first.shape[4], conv_coarse.shape[3], conv_coarse.shape[4]
    half, quarter = width // 2, width // 4
    d2, h2 = depth // 2, height // 2
    part = down_second.shape[4]
    cells = groups * quarter
    vol = volume.reshape(c1 * depth * height, width)
    fine = conv_fine.reshape(27, c1, c1)
    down1 = down_first.reshape(2, 4 * c1, c2)
    middle = conv_middle.reshape(9, 3 * c2, c2)
    shard = jnp.swapaxes(down_second, 3, 4).reshape(8, part, c2)
    pairs = h2 + 1
    coarse_w = conv_coarse.reshape(9, 3 * c3, c4)
    V = pltpu.VMEM
    vmem, away = pl.BlockSpec(memory_space=pltpu.VMEM), pl.BlockSpec(memory_space=pl.ANY)
    dma = pltpu.SemaphoreType.DMA
    result = pl.pallas_call(
        functools.partial(kernel, slabs, groups),
        out_shape=jax.ShapeDtypeStruct((c4, cells), F32),
        in_specs=[vmem, vmem, away, away, vmem, away],
        out_specs=vmem,
        scratch_shapes=[
            V((depth + 2, height + 2, c1, width), F32),
            V((pairs, width, 2 * c1), F32),
            V((2, depth + 2, pairs, half, 8 * c1), BF16),
            V((3, 2, 8 * c1, 4 * c1), BF16),
            V((3, 2, 8 * c1, 4 * c1), BF16),
            V(down1.shape, F32),
            V(down1.shape, BF16),
            V(down1.shape, BF16),
            V(middle.shape, F32),
            V((3, 12 * c2, 2 * c2), BF16),
            V((3, 12 * c2, 2 * c2), BF16),
            V((d2 + 2, h2 + 2, half, c2), F32),
            V((2, d2 + 2, half, 12 * c2), BF16),
            V((h2, d2 * half, c2), F32),
            V((groups,) + shard.shape, F32),
            V(coarse_w.shape, F32),
            V((3, 3 * c3, 2 * c4), BF16),
            V((3, 3 * c3, 2 * c4), BF16),
            V((3, 3 * c3, c4), BF16),
            V((3, 3 * c3, c4), BF16),
            V((groups, quarter, c3), F32),
            V((2, cells + 2 * quarter, 3 * c3), BF16),
            V((cells, c4), F32),
            V((cells, c4), F32),
            V((cells, c4), F32),
            V((cells, c4), F32),
            dma((3,)),
            dma((8,)), dma((8,)), dma((8,)), dma((8,)),
            dma((groups,)), dma((groups,)), dma((groups,)), dma((groups,)), dma((groups,)), dma((groups,)), dma((groups,)), dma((groups,)),
            dma((2,)), dma((2,)),
        ],
        compiler_params=pltpu.CompilerParams(
            collective_id=0, has_side_effects=True, vmem_limit_bytes=60 * 1024 * 1024
        ),
    )(vol, fine, down1, middle, shard, coarse_w)
    return result.reshape(c4, 1, cells)


def solution(mesh):
    placed = (
        P(None, "slab", "grp", None),
        P(),
        P(),
        P(),
        P(None, None, None, None, "grp"),
        P(None, None, None, None, "grp"),
    )
    body = functools.partial(per_device, mesh.shape["slab"], mesh.shape["grp"])
    return jax.shard_map(
        body, mesh=mesh, in_specs=placed, out_specs=P("grp", "slab", None), check_vma=False
    )
```

time: 48.1 us -> 39.1 us (0.81)
  Pallas kernels: 42.3 us -> 37.4 us
  local copies, waits for them, and re-layouts: 5.54 us -> 1.47 us
    pallas_call x1, Pallas kernels: 42.3 us -> 37.4 us  [per_device(): pl.pallas_call(functools.partial(kernel, slabs, groups), out_shape=jax.Sh...]
    unnamed x3 -> x1, local copies, waits for them, and re-layouts: 4.63 us -> 1.47 us
    reshape x1 -> x0, local copies, waits for them, and re-layouts: 0.91 us -> none  [per_device(): shard = down_second.reshape(8 * c2, part).T]
where the time goes in v3:
time: 39.1 us; the launch traced here: 38.9 us
  Pallas kernels  37.4 us (96%)
  local copies, waits for them, and re-layouts  1.47 us (4%)
    pallas_call x1, Pallas kernels, per_device(): pl.pallas_call(functools.partial(kernel, slabs, groups), out_shape=jax.Sh...  37.4 us
    unnamed x1, local copies, waits for them, and re-layouts  1.47 us

profile of v3, /device:TPU:1, one launch (start us, length us, event | category | flops | bytes accessed | tf_op | source)
XLA Modules:
  0.0 38.9 jit_solution(12728793375046507825)
XLA Ops:
  0.0 37.4 %shard_map.64 = f32[128,128]{1,0:T(8,128)} custom-call(f32[1024,128]{1,0:T(8,128)} %bitcast.14, f32[27,64,64]{2,1,0:T(8,128)} %bitcast.13, f32[2,256,128]{2,1,0:T(8,128)} %bitcast.16, f32[9,384,128]{2,1,0:T(8,128)} %bitcast.12, f32[8,64,128]{2,1,0:T(8,128)} %bitcast.17, f32[9,768,128]{2,1,0:T(8,128)} %bitcast.11), custom_call_target="tpu_custom_call" | custom-call | tf_op jit(solution)/shard_map/pallas_call | solution.py:414
  37.4 1.5 %copy.9 = f32[128,1,128]{2,1,0:T(1,128)} copy(f32[128,1,128]{2,1,0:T(1,128)} %bitcast.15) | data formatting | bytes 131072

commit v4 on v3

--- a/solution.py
+++ b/solution.py
@@ -45,9 +45,9 @@
 
 def kernel(
     slabs, groups,
-    vol, fine, down1_hbm, middle_hbm, shard, coarse_hbm,
+    vol_hbm, fine_hbm, down1_hbm, middle_hbm, shard, coarse_hbm,
     out,
-    field, pair, rows, fine_h, fine_l, down1, down1_h, down1_l, middle, middle_h, middle_l,
+    vol, fine, field, pair, rows, fine_h, fine_l, down1, down1_h, down1_l, middle, middle_h, middle_l,
     second, rows2, level2, gathered, coarse_w, edges_h, edges_l, centre_h, centre_l,
     coarse, taps, upward, downward, from_lower, from_upper,
     load_sem, send1, recv1, send2, recv2, wsend, wrecv, xsend, xrecv, fsend, frecv, csend, crecv, psend, precv,
@@ -57,6 +57,9 @@
     half = width // 2
 
     loads = [
+        pltpu.make_async_copy(vol_hbm, vol, load_sem.at[3]),
+        pltpu.make_async_copy(fine_hbm, fine, load_sem.at[4]),
+        pltpu.make_async_copy(shard, gathered.at[g], load_sem.at[5]),
         pltpu.make_async_copy(down1_hbm, down1, load_sem.at[0]),
         pltpu.make_async_copy(middle_hbm, middle, load_sem.at[1]),
         pltpu.make_async_copy(coarse_hbm, coarse_w, load_sem.at[2]),
@@ -67,10 +70,6 @@
     def exists(ds, dg):
         return (s + ds >= 0) & (s + ds < slabs) & (g + dg >= 0) & (g + dg < groups)
 
-    lines = depth * height
-    for r in range(lines):
-        field[1 + r // height, 1 + r % height] = vol[pl.ds(r, chans, stride=lines), :]
-
     barrier = pltpu.get_barrier_semaphore()
     heard = jnp.int32(0)
     for ds, dg in WAYS:
@@ -91,9 +90,19 @@
                 pl.semaphore_signal(barrier, inc=1, device_id=(s, g + sign * dg), device_id_type=MESH)
 
     sibling = s + 1 - 2 * lax.rem(s, 2)
-    across = s + 2 - 4 * lax.rem(s // 2, 2)
-    pl.semaphore_signal(barrier, inc=1, device_id=(across, g), device_id_type=MESH)
-    pl.semaphore_wait(barrier, heard + 1)
+    place = lax.rem(s // 2, 4)
+    crossings = []
+    for hop in (1, 2, 3):
+        low, high = hop % 2, hop // 2
+        step = low * (1 - 2 * lax.rem(place, 2)) + 2 * high * (1 - 2 * (place // 2))
+        crossings.append(s + 2 * step)
+    for peer in crossings:
+        pl.semaphore_signal(barrier, inc=1, device_id=(peer, g), device_id_type=MESH)
+    loads[0].wait()
+    lines = depth * height
+    for r in range(lines):
+        field[1 + r // height, 1 + r % height] = vol[pl.ds(r, chans, stride=lines), :]
+    pl.semaphore_wait(barrier, heard + len(crossings))
 
     def part(way, size, offset):
         if way == 0:
@@ -147,14 +156,14 @@
     first = halo(field, 1, field, send1, recv1)
 
     taps_of = shard.shape[0]
-    parity, bit = lax.rem(s, 2), lax.rem(s // 2, 2)
-    quarter_taps = pl.ds((parity * 2 + bit) * (taps_of // 4), taps_of // 4)
-    half_taps = pl.ds(parity * (taps_of // 2), taps_of // 2)
+    parity = lax.rem(s, 2)
+    eighth = pl.ds(parity * 4 + place, 1)
+    half_taps = pl.ds(parity * 4, 4)
     spread, crossed, forward = [], [], []
     for j in range(1, groups):
         copy = pltpu.make_async_remote_copy(
-            src_ref=shard.at[quarter_taps],
-            dst_ref=gathered.at[g, quarter_taps],
+            src_ref=shard.at[eighth],
+            dst_ref=gathered.at[g, eighth],
             send_sem=wsend.at[j],
             recv_sem=wrecv.at[j],
             device_id=(s, lax.rem(g + j, groups)),
@@ -163,23 +172,26 @@
         copy.start()
         spread.append(copy)
 
-    def hand_on(arrived, out_copies, piece, sends, recvs, peer):
+    def hand_on(arrived, out_copies, piece, sends, recvs, peers):
         for j in range(1, groups):
-            arrived[j - 1].wait_recv()
+            for copy in arrived[j - 1]:
+                copy.wait_recv()
             source = lax.rem(g + groups - j, groups)
-            copy = pltpu.make_async_remote_copy(
-                src_ref=gathered.at[source, piece],
-                dst_ref=gathered.at[source, piece],
-                send_sem=sends.at[j],
-                recv_sem=recvs.at[j],
-                device_id=(peer, g),
-                device_id_type=MESH,
-            )
-            copy.start()
-            out_copies.append(copy)
-
-    gathered[pl.ds(g, 1)] = shard[...][None]
-
+            made = []
+            for k, peer in enumerate(peers):
+                copy = pltpu.make_async_remote_copy(
+                    src_ref=gathered.at[source, piece],
+                    dst_ref=gathered.at[source, piece],
+                    send_sem=sends.at[j, k],
+                    recv_sem=recvs.at[j, k],
+                    device_id=(peer, g),
+                    device_id_type=MESH,
+                )
+                copy.start()
+                made.append(copy)
+            out_copies.append(made)
+
+    loads[1].wait()
     blank = jnp.zeros((chans, 2 * chans), BF16)
     nothing = jnp.zeros((chans, chans), F32)
     for a in range(3):
@@ -202,7 +214,7 @@
     pairs = height // 2 + 1
     blocks = height // 2
     d2, h2, c2 = depth // 2, blocks, down1.shape[2]
-    for load in loads:
+    for load in loads[2:]:
         load.wait()
     for a in range(2):
         down1_h[a], down1_l[a] = split(down1[a])
@@ -254,6 +266,7 @@
     for p in (0, blocks):
         build(p)
         convolve(p)
+    hand_on([[c] for c in spread], crossed, eighth, xsend, xrecv, crossings)
     ones = [gelu(t).reshape(d2, 2, half, 4 * chans) for t in totals]
     total = None
     for a in range(2):
@@ -263,7 +276,6 @@
     for h in range(h2):
         second[1 : d2 + 1, 1 + h] = total[h]
     again = halo(second, 1, second, send2, recv2)
-    hand_on(spread, crossed, quarter_taps, xsend, xrecv, across)
 
     def widen(h):
         @pl.loop(0, d2 + 2)
@@ -290,7 +302,7 @@
     for a in range(3):
         sides[0] = plus(sides[0], middle_term(a, 0, k3, 0, c2))
         sides[1] = plus(sides[1], middle_term(a, 3 * k3, 4 * k3, c2, 2 * c2))
-    hand_on(crossed, forward, half_taps, fsend, frecv, sibling)
+    hand_on(crossed, forward, half_taps, fsend, frecv, [sibling])
     for h in range(h2):
         level2[h] = gelu(total[:, h * c2 : (h + 1) * c2] + sides[h])
     quarter = half // 2
@@ -302,8 +314,8 @@
         axis=1,
     )
     lhs = stacked(lhs)
-    for copy in forward:
-        copy.wait_recv()
+    for made in forward:
+        made[0].wait_recv()
     weights = jnp.concatenate(
         [gathered[:, t].reshape(groups * shard.shape[1], c2) for t in range(taps_of)], axis=1
     )
@@ -382,7 +394,7 @@
 
     arrive(first, False)
     arrive(again, False)
-    for copy in spread + crossed + forward + sent:
+    for copy in spread + sum(crossed + forward, []) + sent:
         copy.wait_send()
 
     @pl.when(exists(1, 0))
@@ -414,9 +426,11 @@
     result = pl.pallas_call(
         functools.partial(kernel, slabs, groups),
         out_shape=jax.ShapeDtypeStruct((c4, cells), F32),
-        in_specs=[vmem, vmem, away, away, vmem, away],
+        in_specs=[away] * 6,
         out_specs=vmem,
         scratch_shapes=[
+            V(vol.shape, F32),
+            V(fine.shape, F32),
             V((depth + 2, height + 2, c1, width), F32),
             V((pairs, width, 2 * c1), F32),
             V((2, depth + 2, pairs, half, 8 * c1), BF16),
@@ -443,9 +457,9 @@
             V((cells, c4), F32),
             V((cells, c4), F32),
             V((cells, c4), F32),
-            dma((3,)),
+            dma((6,)),
             dma((8,)), dma((8,)), dma((8,)), dma((8,)),
-            dma((groups,)), dma((groups,)), dma((groups,)), dma((groups,)), dma((groups,)), dma((groups,)), dma((groups,)), dma((groups,)),
+            dma((groups,)), dma((groups,)), dma((groups, 3)), dma((groups, 3)), dma((groups, 1)), dma((groups, 1)), dma((groups,)), dma((groups,)),
             dma((2,)), dma((2,)),
         ],
         compiler_params=pltpu.CompilerParams(

time: 39.1 us -> 40.7 us (1.041)
  Pallas kernels: 37.4 us -> 39.1 us
    pallas_call x1, Pallas kernels: 37.4 us -> 39.1 us  [per_device(): pl.pallas_call(functools.partial(kernel, slabs, groups), out_shape=jax.Sh...]
where the time goes in v4:
time: 40.7 us; the launch traced here: 40.6 us
  Pallas kernels  39.1 us (96%)
  local copies, waits for them, and re-layouts  1.47 us (4%)
    pallas_call x1, Pallas kernels, per_device(): pl.pallas_call(functools.partial(kernel, slabs, groups), out_shape=jax.Sh...  39.1 us
    unnamed x1, local copies, waits for them, and re-layouts  1.47 us

profile of v4, /device:TPU:1, one launch (start us, length us, event | category | flops | bytes accessed | tf_op | source)
XLA Modules:
  0.0 40.6 jit_solution(173870518629124729)
XLA Ops:
  0.0 39.1 %shard_map.64 = f32[128,128]{1,0:T(8,128)} custom-call(f32[1024,128]{1,0:T(8,128)} %bitcast.14, f32[27,64,64]{2,1,0:T(8,128)} %bitcast.13, f32[2,256,128]{2,1,0:T(8,128)} %bitcast.16, f32[9,384,128]{2,1,0:T(8,128)} %bitcast.12, f32[8,64,128]{2,1,0:T(8,128)} %bitcast.17, f32[9,768,128]{2,1,0:T(8,128)} %bitcast.11), custom_call_target="tpu_custom_call" | custom-call | tf_op jit(solution)/shard_map/pallas_call | solution.py:426
  39.1 1.5 %copy.9 = f32[128,1,128]{2,1,0:T(1,128)} copy(f32[128,1,128]{2,1,0:T(1,128)} %bitcast.15) | data formatting | bytes 131072

commit v5 on v4

--- a/solution.py
+++ b/solution.py
@@ -90,12 +90,8 @@
                 pl.semaphore_signal(barrier, inc=1, device_id=(s, g + sign * dg), device_id_type=MESH)
 
     sibling = s + 1 - 2 * lax.rem(s, 2)
-    place = lax.rem(s // 2, 4)
-    crossings = []
-    for hop in (1, 2, 3):
-        low, high = hop % 2, hop // 2
-        step = low * (1 - 2 * lax.rem(place, 2)) + 2 * high * (1 - 2 * (place // 2))
-        crossings.append(s + 2 * step)
+    place = lax.rem(s // 2, 2)
+    crossings = [s + 2 - 4 * place]
     for peer in crossings:
         pl.semaphore_signal(barrier, inc=1, device_id=(peer, g), device_id_type=MESH)
     loads[0].wait()
@@ -157,13 +153,13 @@
 
     taps_of = shard.shape[0]
     parity = lax.rem(s, 2)
-    eighth = pl.ds(parity * 4 + place, 1)
-    half_taps = pl.ds(parity * 4, 4)
+    fourth = pl.ds((parity * 2 + place) * (taps_of // 4), taps_of // 4)
+    half_taps = pl.ds(parity * (taps_of // 2), taps_of // 2)
     spread, crossed, forward = [], [], []
     for j in range(1, groups):
         copy = pltpu.make_async_remote_copy(
-            src_ref=shard.at[eighth],
-            dst_ref=gathered.at[g, eighth],
+            src_ref=shard.at[fourth],
+            dst_ref=gathered.at[g, fourth],
             send_sem=wsend.at[j],
             recv_sem=wrecv.at[j],
             device_id=(s, lax.rem(g + j, groups)),
@@ -266,7 +262,6 @@
     for p in (0, blocks):
         build(p)
         convolve(p)
-    hand_on([[c] for c in spread], crossed, eighth, xsend, xrecv, crossings)
     ones = [gelu(t).reshape(d2, 2, half, 4 * chans) for t in totals]
     total = None
     for a in range(2):
@@ -276,6 +271,7 @@
     for h in range(h2):
         second[1 : d2 + 1, 1 + h] = total[h]
     again = halo(second, 1, second, send2, recv2)
+    hand_on([[c] for c in spread], crossed, fourth, xsend, xrecv, crossings)
 
     def widen(h):
         @pl.loop(0, d2 + 2)

time: 40.7 us -> 37.8 us (0.929)
  Pallas kernels: 39.1 us -> 36.2 us
    pallas_call x1, Pallas kernels: 39.1 us -> 36.2 us  [per_device(): pl.pallas_call(functools.partial(kernel, slabs, groups), out_shape=jax.Sh...]
where the time goes in v5:
time: 37.8 us; the launch traced here: 37.6 us
  Pallas kernels  36.2 us (96%)
  local copies, waits for them, and re-layouts  1.47 us (4%)
    pallas_call x1, Pallas kernels, per_device(): pl.pallas_call(functools.partial(kernel, slabs, groups), out_shape=jax.Sh...  36.2 us
    unnamed x1, local copies, waits for them, and re-layouts  1.47 us

profile of v5, /device:TPU:1, one launch (start us, length us, event | category | flops | bytes accessed | tf_op | source)
XLA Modules:
  0.0 37.6 jit_solution(3728488284318303368)
XLA Ops:
  0.0 36.2 %shard_map.64 = f32[128,128]{1,0:T(8,128)} custom-call(f32[1024,128]{1,0:T(8,128)} %bitcast.14, f32[27,64,64]{2,1,0:T(8,128)} %bitcast.13, f32[2,256,128]{2,1,0:T(8,128)} %bitcast.16, f32[9,384,128]{2,1,0:T(8,128)} %bitcast.12, f32[8,64,128]{2,1,0:T(8,128)} %bitcast.17, f32[9,768,128]{2,1,0:T(8,128)} %bitcast.11), custom_call_target="tpu_custom_call" | custom-call | tf_op jit(solution)/shard_map/pallas_call | solution.py:422
  36.2 1.5 %copy.9 = f32[128,1,128]{2,1,0:T(1,128)} copy(f32[128,1,128]{2,1,0:T(1,128)} %bitcast.15) | data formatting | bytes 131072
